TPU v7x, 32 devices: a whole 2x2x4 slice. The times are simulated.
32 devices in a mesh: seq: 8 (over z, core), fsdp: 4 (over y, x).
Axes of the slice: x: 2, y: 2, z: 4, core: 2. Of those that a mesh axis runs over, the one named last changes fastest.
Arguments:
- tokens: bfloat16 [1024, 8192], P('seq', 'fsdp'), may hold values from -6 to 6
- norm_gain: float32 [8192], replicated, may hold values from 0.25 to 1.75
- gate_proj: bfloat16 [8192, 8192], P('seq', 'fsdp'), may hold values from -0.0625 to 0.0625
- value_proj: bfloat16 [8192, 8192], P('seq', 'fsdp'), may hold values from -0.0625 to 0.0625
- step_proj: bfloat16 [8192, 128], P('seq', 'fsdp'), may hold values from -0.0625 to 0.0625
- state_proj: bfloat16 [8192, 4, 256], P('seq'), may hold values from -0.0625 to 0.0625
- conv_value: float32 [4, 8192], P(None, 'fsdp'), may hold values from -3 to 3
- conv_state: float32 [4, 4, 256], replicated, may hold values from -3 to 3
- step_bias: float32 [128], P('fsdp'), may hold values from -1 to 1
- decay_rate: float32 [128], P('fsdp'), may hold values from 0.00048828125 to 0.1
- skip_gain: float32 [128], P('fsdp'), may hold values from 0.5 to 1.5
- mix_gain: float32 [8192], P('fsdp'), may hold values from 0.25 to 1.75
- out_proj: bfloat16 [8192, 8192], P('fsdp', 'seq'), may hold values from -0.09375 to 0.09375
- doc_lengths: int32 [16], replicated, may hold values from 1 to 512, 1024 in all
Outputs:
- layer_out: bfloat16 [1024, 8192], P('seq', 'fsdp')
Inputs may be any that keep to these rules, and one draw needn't show every extreme that they name: `doc_lengths`: the longest document has exactly 512 tokens, so it spans many stretches; the lengths sum to 1024.
All inputs are finite; a program needn't handle non-finite values.
Results may differ from a plain program's by a relative error of at most 0.014.
Values may be sent and summed in bfloat16 or wider, within the bound.
No kernel may reach another device: no remote copies, remote signals or barrier semaphores. Data moves between devices by JAX's collectives and lax.ppermute only.
A program may use at most 128 MiB of HBM per device.

v0:
```python
import jax
import jax.numpy as jnp
from jax import lax
from jax.experimental import pallas as pl
from jax.experimental.pallas import tpu as pltpu
from jax.sharding import PartitionSpec as P

H = 128
HEAD_DIM = 64
N = 128
G = 4


EPSILON = 1e-05
PRECISE = lax.Precision.HIGHEST


def from_behind(value, axis, steps):
    count = lax.axis_size(axis)
    leading, last = (max(0, -steps), min(count, count - steps))
    return lax.ppermute(value, axis, [(source, source + steps) for source in range(leading, last)])


def partner(block, axis, distance):
    count = lax.axis_size(axis)
    route = []
    for low in range(count):
        high = low | 1 << distance
        if high != low and high < count:
            route += [(low, high), (high, low)]
    return lax.ppermute(block, axis, route)


def by_stretch(
    tokens,
    norm_gain,
    gate_proj,
    value_proj,
    step_proj,
    state_proj,
    conv_value,
    conv_state,
    step_bias,
    decay_rate,
    skip_gain,
    mix_gain,
    out_proj,
    doc_lengths,
):
    span_rows = tokens.shape[0]
    seq_index = lax.axis_index("seq")
    fsdp_index = lax.axis_index("fsdp")
    head_count = step_bias.shape[0]
    inner_width = gate_proj.shape[1]
    group_devices = lax.axis_size("fsdp") // G
    group_index = fsdp_index // group_devices
    gathered = lax.all_gather(tokens, "fsdp", axis=1, tiled=True)
    as_float = gathered.astype(jnp.float32)
    normed = (
        as_float
        * lax.rsqrt(jnp.mean(as_float * as_float, axis=1, keepdims=True) + EPSILON)
        * norm_gain
    ).astype(jnp.bfloat16)
    state_cols = lax.dynamic_index_in_dim(state_proj, group_index, 1, keepdims=False)
    stacked = jnp.concatenate([gate_proj, value_proj, state_cols, step_proj], axis=1)
    spread = lax.all_to_all(normed, "seq", split_axis=1, concat_axis=0, tiled=True)
    summed = lax.psum_scatter(
        jnp.dot(spread, stacked, preferred_element_type=jnp.float32),
        "seq",
        scatter_dimension=0,
        tiled=True,
    )
    gate = summed[:, :inner_width]
    values = summed[:, inner_width : 2 * inner_width]
    states = summed[:, 2 * inner_width : 2 * inner_width + 2 * N]
    raw_step = summed[:, 2 * inner_width + 2 * N :]
    raw_mix = jnp.concatenate([values, states], axis=1).astype(jnp.bfloat16)
    tail_rows = from_behind(raw_mix[span_rows - 3 :], "seq", 1)
    extended = jnp.concatenate([tail_rows, raw_mix], axis=0)
    starts = jnp.cumsum(doc_lengths) - doc_lengths
    span_start = seq_index * span_rows
    positions = span_start - 3 + jnp.arange(span_rows + 3, dtype=jnp.int32)
    segment_ext = jnp.sum(starts[None, :] <= positions[:, None], axis=1) - 1
    segment = segment_ext[3:]
    taps = jnp.concatenate(
        [conv_value, lax.dynamic_index_in_dim(conv_state, group_index, 1, keepdims=False)], axis=1
    )
    convolved = jnp.zeros((span_rows, taps.shape[1]), jnp.float32)
    for offset in range(4):
        same_doc = segment_ext[offset : offset + span_rows] == segment
        convolved = (
            convolved
            + jnp.where(
                same_doc[:, None], extended[offset : offset + span_rows].astype(jnp.float32), 0.0
            )
            * taps[offset]
        )
    rounded = lax.optimization_barrier(jax.nn.silu(convolved).astype(jnp.bfloat16))
    activated = rounded.astype(jnp.float32)
    inputs = activated[:, :inner_width].reshape(span_rows, head_count, HEAD_DIM)
    in_map = activated[:, inner_width : inner_width + N]
    out_map = activated[:, inner_width + N :]
    in_half = rounded[:, inner_width : inner_width + N]
    out_half = rounded[:, inner_width + N :]
    step_size = jax.nn.softplus(raw_step + step_bias)
    log_decay = -decay_rate * step_size
    cumulative = jnp.cumsum(log_decay, axis=0)
    order = jnp.arange(span_rows)
    causal = (segment[:, None] == segment[None, :]) & (order[:, None] >= order[None, :])
    gaps = cumulative.T[:, :, None] - cumulative.T[:, None, :]
    decay = jnp.exp(jnp.where(causal[None], gaps, -jnp.inf))
    scores = jnp.dot(out_half, in_half.T, preferred_element_type=jnp.float32)
    mixing = decay * scores[None] * step_size.T[:, None, :]
    intra = jnp.einsum("hts,shp->thp", mixing, inputs, precision=PRECISE)
    last_segment = segment[span_rows - 1]
    prior_segment = segment_ext[2]
    in_last = segment == last_segment
    to_end = (
        jnp.where(in_last[:, None], jnp.exp(cumulative[span_rows - 1][None, :] - cumulative), 0.0)
        * step_size
    )
    local_state = jnp.einsum("sh,shp,sn->hpn", to_end, inputs, in_map, precision=PRECISE)
    passing = jnp.where(last_segment == prior_segment, jnp.exp(cumulative[span_rows - 1]), 0.0)
    empty = jnp.zeros_like(local_state)

    def relay(turn, incoming):
        return from_behind(
            (passing[:, None, None] * incoming + local_state).astype(jnp.bfloat16), "seq", 1
        ).astype(jnp.float32)

    incoming = lax.fori_loop(0, lax.axis_size("seq") - 1, relay, empty)
    carried = jnp.where((segment == prior_segment)[:, None], jnp.exp(cumulative), 0.0)
    from_state = (
        jnp.einsum("tn,hpn->thp", out_map, incoming, precision=PRECISE) * carried[:, :, None]
    )
    outputs = intra + from_state + skip_gain[None, :, None] * inputs
    gated = outputs.reshape(span_rows, inner_width) * jax.nn.silu(gate)
    squares = jnp.sum(gated * gated, axis=1)
    for bit in range(group_devices.bit_length() - 1):
        squares = squares + partner(squares, "fsdp", bit)
    scaled = (
        gated * lax.rsqrt(squares[:, None] / (H * HEAD_DIM // G) + EPSILON) * mix_gain
    ).astype(jnp.bfloat16)
    terms = jnp.dot(
        scaled,
        lax.all_gather(out_proj, "seq", axis=1, tiled=True),
        preferred_element_type=jnp.float32,
    )
    mixed = lax.psum_scatter(
        terms.astype(jnp.bfloat16), "fsdp", scatter_dimension=1, tiled=True
    ).astype(jnp.float32)
    return (tokens.astype(jnp.float32) + mixed).astype(jnp.bfloat16)


VMEM_BYTES = 56 << 20


def swap_cores(value):
    count = lax.axis_size("seq")
    return lax.ppermute(value, "seq", [(place, place ^ 1) for place in range(count)])


def next_chip(value, away=1):
    count = lax.axis_size("seq")
    route = [(place, (place + 2 * away) % count) for place in range(count)]
    return lax.ppermute(value, "seq", route)


def flip_fsdp(value, bits):
    count = lax.axis_size("fsdp")
    return lax.ppermute(value, "fsdp", [(place, place ^ bits) for place in range(count)])


def share_partials(pieces, value_proj, gate_proj, small, where, chips, width):
    depth, count = pieces[0].shape[1], pieces[0].shape[0]
    rows = count // (2 * chips)
    number = len(pieces)
    tall = number * count
    projections = [value for value in (value_proj, gate_proj) if value is not None]
    thin_inputs = [] if small is None else [small]
    thin_rows = 0 if small is None else number * (rows + rows // 2)
    thin_width = 128 if small is None else small.shape[1]
    total_rows = len(projections) * tall + thin_rows

    def body(where, *refs):
        row_refs, refs = refs[:number], refs[number:]
        weight_refs, refs = refs[: len(projections)], refs[len(projections) :]
        lent_ref, kept_ref, thin = refs[-3:]
        index, core = pl.program_id(0), where[1]
        chip = lax.rem(where[0] + chips - index, chips)
        first = core == 0

        if small is not None:

            @pl.when(index == 0)
            def _():
                for place in range(number):
                    thin[place * count : (place + 1) * count] = jnp.dot(
                        row_refs[place][...], refs[0][...], preferred_element_type=jnp.float32
                    ).astype(jnp.bfloat16)

            for out_ref, own in ((lent_ref, 1 - core), (kept_ref, core)):
                for place in range(number):
                    at = place * count + (own * chips + chip) * rows
                    to = tall + place * rows
                    out_ref[0, to : to + rows] = thin[
                        pl.ds(pl.multiple_of(at, rows), rows), : thin_width - 128
                    ]
                    to = tall + number * rows + place * rows // 2
                    halves = [
                        thin[
                            pl.ds(pl.multiple_of(at + part * rows // 2, rows // 2), rows // 2),
                            thin_width - 128 :,
                        ]
                        for part in range(2)
                    ]
                    out_ref[0, to : to + rows // 2] = jnp.concatenate(halves, axis=1)

        for which, weight_ref in enumerate(weight_refs):
            base = which * (tall + thin_rows)
            for place in range(number):
                both = jnp.dot(
                    row_refs[place][...], weight_ref[...], preferred_element_type=jnp.float32
                ).astype(jnp.bfloat16)
                at = slice(base + place * count, base + (place + 1) * count)
                kept_ref[0, at] = jnp.where(first, both[:, :width], both[:, width:])
                lent_ref[0, at] = jnp.where(first, both[:, width:], both[:, :width])

    out = jax.ShapeDtypeStruct((chips, total_rows, width), jnp.bfloat16)
    return pl.pallas_call(
        body,
        out_shape=[out, out],
        grid_spec=pltpu.PrefetchScalarGridSpec(
            num_scalar_prefetch=1,
            grid=(chips,),
            in_specs=[pl.BlockSpec((count, depth), lambda i, where: (0, 0)) for _ in pieces]
            + [
                pl.BlockSpec(
                    (depth, 2 * width), lambda i, where: (0, lax.rem(where[0] + chips - i, chips))
                )
                for _ in projections
            ]
            + [pl.BlockSpec(value.shape, lambda i, where: (0, 0)) for value in thin_inputs],
            out_specs=[pl.BlockSpec((1, total_rows, width), lambda i, where: (i, 0, 0))] * 2,
            scratch_shapes=[
                pltpu.VMEM((16 if small is None else tall, thin_width), jnp.bfloat16)
            ],
        ),
        compiler_params=pltpu.CompilerParams(vmem_limit_bytes=VMEM_BYTES),
        name="share_partials",
    )(where, *pieces, *projections, *thin_inputs)


def add_up(*terms):
    total = terms[0].astype(jnp.float32)
    for term in terms[1:]:
        total = total + term.astype(jnp.float32)
    return total


def ring_reduce(kept, lent):
    got = swap_cores(lent)
    chips = kept.shape[0]
    passed = []
    for step in range(1, chips):
        sent = add_up(kept[step], got[step], *passed).astype(jnp.bfloat16)
        passed = [next_chip(sent)]
    return kept, got, passed[0]


def scan_heads(order, trios, groups, thin, thin_swapped, ages, taps, state_taps, bias, rate, skip, sizes):
    stretches, rows, quarters, width = sizes
    span = rows * quarters
    tokens = stretches * span
    count = stretches * rows
    half = rows // 2
    chips = stretches // 2
    heads = width // HEAD_DIM
    flat = [value for trio in trios for value in trio]
    number = len(flat)

    def body(order, *refs):
        trio_refs, refs = refs[:number], refs[number:]
        thin_ref, swapped_ref, ages_ref, taps_ref, state_taps_ref, bias_ref = refs[:6]
        rate_ref, skip_ref, out_ref, values, maps, steps, state = refs[6:]
        first_head, chip, core = (order[quarters + place] for place in range(3))
        values[:8] = jnp.zeros((8, width), jnp.float32)
        maps[:8] = jnp.zeros((8, 2 * N), jnp.float32)

        def place_rows(stretch, carry):
            for group, members in enumerate(groups):
                kept, got, last = trio_refs[3 * group : 3 * group + 3]
                for place, k in enumerate(members):
                    at = pl.multiple_of(place * count + stretch * rows, rows)
                    to = pl.multiple_of(stretch * span + order[k] * rows, rows)
                    total = (
                        kept[0, pl.ds(at, rows), :].astype(jnp.float32)
                        + got[0, pl.ds(at, rows), :].astype(jnp.float32)
                        + last[pl.ds(at, rows), :].astype(jnp.float32)
                    )
                    values[pl.ds(to + 8, rows), :] = total.astype(jnp.bfloat16).astype(
                        jnp.float32
                    )
            return carry

        lax.fori_loop(0, stretches, place_rows, 0)
        for source, own_core in ((thin_ref, core), (swapped_ref, 1 - core)):
            for away in range(chips):
                stretch = own_core * chips + lax.rem(chip + chips - away, chips)
                base = 0
                for members in groups:
                    for place, k in enumerate(members):
                        to = pl.multiple_of(stretch * span + order[k] * rows, rows)
                        at = base + place * rows
                        maps[pl.ds(to + 8, rows), :] = source[away, at : at + rows].astype(
                            jnp.float32
                        )
                        at = base + len(members) * rows + place * half
                        for part in range(2):
                            steps[pl.ds(pl.multiple_of(to + part * half, half), half), :] = source[
                                away, at : at + half, part * 128 : (part + 1) * 128
                            ].astype(jnp.float32)
                    base += len(members) * (rows + half)
        state[...] = jnp.zeros_like(state)
        row = lax.broadcasted_iota(jnp.int32, (span, span), 0)
        gap = row - lax.broadcasted_iota(jnp.int32, (span, span), 1)
        lower = jnp.where(gap >= 0, 1.0, 0.0)
        here = lax.broadcasted_iota(jnp.int32, (span, 1), 0)
        head_of = lax.broadcasted_iota(jnp.int32, (1, width), 1) // HEAD_DIM

        def by_head(columns):
            wide = jnp.broadcast_to(columns[:, 0:1], (columns.shape[0], width))
            for head in range(1, heads):
                wide = jnp.where(head_of == head, columns[:, head : head + 1], wide)
            return wide

        def convolve(source, gains, start, age):
            block = source[pl.ds(start, span + 8), :]
            total = block[8:] * gains[3:4]
            for lag in range(1, 4):
                total = total + jnp.where(age >= lag, block[8 - lag : 8 - lag + span], 0.0) * gains[
                    3 - lag : 4 - lag
                ]
            return (total * jax.nn.sigmoid(total)).astype(jnp.bfloat16)

        def chunk(index, carry):
            start = pl.multiple_of(index * span, span)
            age = ages_ref[pl.ds(start, span), :]
            last_age = age[span - 1 :]
            inputs = convolve(values, taps_ref[...], start, age)
            both = convolve(maps, state_taps_ref[...], start, age)
            in_map, out_map = both[:, :N], both[:, N:]
            raw = pltpu.roll(steps[pl.ds(start, span), :], lax.rem(128 - first_head, 128), 1)
            raw = raw + bias_ref[...]
            size = jnp.maximum(raw, 0.0) + jnp.log1p(jnp.exp(-jnp.abs(raw)))
            total = jnp.dot(
                lower,
                -rate_ref[...] * size,
                precision=PRECISE,
                preferred_element_type=jnp.float32,
            )
            total_rows, size_rows = total.T, size.T
            scores = lax.dot_general(
                out_map, in_map, (((1,), (1,)), ((), ())), preferred_element_type=jnp.float32
            )
            near = (gap >= 0) & (gap <= age)
            history = jnp.zeros((span, width), jnp.float32)
            for head in range(heads):
                decay = jnp.exp(
                    jnp.where(
                        near, total[:, head : head + 1] - total_rows[head : head + 1], -jnp.inf
                    )
                )
                mixing = (decay * scores * size_rows[head : head + 1]).astype(jnp.bfloat16)
                part = jnp.dot(mixing, inputs, preferred_element_type=jnp.float32)
                history = jnp.where(head_of == head, part, history)
            old = state[...]
            carried = by_head(jnp.where(age > here, jnp.exp(total), 0.0))
            history = history + carried * jnp.dot(
                out_map, old.astype(jnp.bfloat16), preferred_element_type=jnp.float32
            )
            wide = inputs.astype(jnp.float32)
            out_ref[pl.ds(start, span), :] = history + skip_ref[...] * wide
            end = total[span - 1 :]
            to_end = by_head(
                jnp.where(span - 1 - here <= last_age, jnp.exp(end - total), 0.0) * size
            )
            keep = by_head(jnp.where(last_age >= span, jnp.exp(end), 0.0))
            state[...] = keep * old + lax.dot_general(
                in_map,
                (wide * to_end).astype(jnp.bfloat16),
                (((0,), (0,)), ((), ())),
                preferred_element_type=jnp.float32,
            )
            return carry

        lax.fori_loop(0, stretches, chunk, 0)

    whole = lambda value: pl.BlockSpec(value.shape, lambda i, order: (0,) * value.ndim)
    trio_specs = [
        pl.BlockSpec((1,) + value.shape[1:], lambda i, order: (0, 0, 0))
        if value.ndim == 3
        else whole(value)
        for value in flat
    ]
    rest = (thin, thin_swapped, ages, taps, state_taps, bias, rate, skip)
    return pl.pallas_call(
        body,
        out_shape=jax.ShapeDtypeStruct((tokens, width), jnp.float32),
        grid_spec=pltpu.PrefetchScalarGridSpec(
            num_scalar_prefetch=1,
            grid=(1,),
            in_specs=trio_specs + [whole(value) for value in rest],
            out_specs=pl.BlockSpec((tokens, width), lambda i, order: (0, 0)),
            scratch_shapes=[
                pltpu.VMEM((tokens + 8, width), jnp.float32),
                pltpu.VMEM((tokens + 8, 2 * N), jnp.float32),
                pltpu.VMEM((tokens, 128), jnp.float32),
                pltpu.VMEM((N, width), jnp.float32),
            ],
        ),
        compiler_params=pltpu.CompilerParams(vmem_limit_bytes=VMEM_BYTES),
        name="scan_heads",
    )(order, *flat, *rest)


def gate_outputs(order, outputs, trios, groups, offsets, sizes):
    stretches, rows, quarters, width = sizes
    count, half, chips = stretches * rows, rows // 2, stretches // 2
    flat = [value for trio in trios for value in trio]
    number = len(flat)

    def body(order, *refs):
        trio_refs, outputs_ref, parts = refs[:number], refs[number], refs[number + 1 :]
        core = order[quarters + 2]

        def one_chip(chip, carry):
            for role, stretch in enumerate((2 * chip + core, 2 * chip + 1 - core)):
                for group, members in enumerate(groups):
                    kept, got, last = trio_refs[3 * group : 3 * group + 3]
                    for place, k in enumerate(members):
                        at = offsets[group] + place * count + stretch * rows
                        at = pl.ds(pl.multiple_of(at, 16), rows)
                        gate = (
                            kept[0, at, :].astype(jnp.float32)
                            + got[0, at, :].astype(jnp.float32)
                            + last[at, :].astype(jnp.float32)
                        )
                        value = (
                            outputs_ref[stretch, order[k]] * gate * jax.nn.sigmoid(gate)
                        ).astype(jnp.bfloat16)
                        for part in range(2):
                            parts[2 * role + part][chip, order[k]] = value[
                                part * half : (part + 1) * half
                            ]
            return carry

        lax.fori_loop(0, chips, one_chip, 0)

    whole = lambda shape: pl.BlockSpec(shape, lambda i, order: (0,) * len(shape))
    shape = (chips, quarters, half, width)
    return pl.pallas_call(
        body,
        out_shape=[jax.ShapeDtypeStruct(shape, jnp.bfloat16)] * 4,
        grid_spec=pltpu.PrefetchScalarGridSpec(
            num_scalar_prefetch=1,
            grid=(1,),
            in_specs=[
                whole((1,) + value.shape[1:] if value.ndim == 3 else value.shape)
                for value in flat
            ]
            + [whole((stretches, quarters, rows, width))],
            out_specs=[whole(shape)] * 4,
        ),
        compiler_params=pltpu.CompilerParams(vmem_limit_bytes=VMEM_BYTES),
        name="gate_outputs",
    )(order, *flat, outputs.reshape(stretches, quarters, rows, width))


def mix_channels(order, near, far, away, so_far, gains, own_proj, other_proj, sizes):
    stretches, rows, quarters, width = sizes
    half, chips = rows // 2, stretches // 2
    count = near.shape[1]
    channels, columns = own_proj.shape
    last = so_far is not None
    so_far = list(so_far) if last else []

    def owner_of(i, order):
        chip, core = order[quarters + 1], order[quarters + 2]
        return 2 * lax.rem(chip + chips - away - i // 2, chips) + lax.rem(core + i, 2)

    def body(order, near_ref, far_ref, gains_ref, own_ref, other_ref, *refs):
        before, refs = refs[: len(so_far)], refs[len(so_far) :]
        total, squares = refs[-2:] if last else refs
        index = pl.program_id(0)

        @pl.when(index == 0)
        def _():
            total[...] = before[0][...] if last else jnp.zeros_like(total)
            squares[...] = before[1][...] if last else jnp.zeros_like(squares)

        block = jnp.where(index < 2, near_ref[0], far_ref[0]).astype(jnp.float32)
        squares[...] += jnp.broadcast_to(
            jnp.sum(block * block, axis=1, keepdims=True), squares.shape
        )
        gained = (block * gains_ref[pl.ds(owner_of(index, order), 1), :]).astype(jnp.bfloat16)
        for side, weights_ref in enumerate((own_ref, other_ref)):
            total[:, side * columns : (side + 1) * columns] += jnp.dot(
                gained, weights_ref[...], preferred_element_type=jnp.float32
            )
        if last:
            rounded = refs[4]

            @pl.when(index == pl.num_programs(0) - 1)
            def _():
                factor = lax.rsqrt(squares[:, :1] / channels + EPSILON)
                rounded[...] = (total[...] * factor).astype(jnp.bfloat16)
                left_kept, left_sent, right_kept, right_sent = refs[:4]
                for k in range(4):
                    for chip in range(chips):
                        at = pl.multiple_of((chip * quarters + order[k]) * half, half)
                        value = rounded[pl.ds(at, half), :]
                        (left_sent if k % 2 else left_kept)[k // 2, chip] = value[:, :columns]
                        (right_sent if k // 2 else right_kept)[k % 2, chip] = value[:, columns:]

    whole = lambda shape: pl.BlockSpec(shape, lambda i, order: (0,) * len(shape))
    sums = [
        jax.ShapeDtypeStruct((count, 2 * columns), jnp.float32),
        jax.ShapeDtypeStruct((count, 128), jnp.float32),
    ]
    part = jax.ShapeDtypeStruct((2, chips, half, columns), jnp.bfloat16)
    outs = [part] * 4 if last else sums
    scratch = [
        pltpu.VMEM((count, 2 * columns), jnp.bfloat16),
        *(pltpu.VMEM(value.shape, value.dtype) for value in sums),
    ]
    weights_spec = pl.BlockSpec((width, columns), lambda i, order: (owner_of(i, order), 0))
    return pl.pallas_call(
        body,
        out_shape=outs,
        grid_spec=pltpu.PrefetchScalarGridSpec(
            num_scalar_prefetch=1,
            grid=(4,),
            in_specs=[
                pl.BlockSpec((1, count, width), lambda i, order: (jnp.minimum(i, 1), 0, 0)),
                pl.BlockSpec((1, count, width), lambda i, order: (jnp.maximum(i - 2, 0), 0, 0)),
                whole(gains.shape),
                weights_spec,
                weights_spec,
            ]
            + [whole(value.shape) for value in so_far],
            out_specs=[whole(value.shape) for value in outs],
            scratch_shapes=scratch if last else [],
        ),
        compiler_params=pltpu.CompilerParams(vmem_limit_bytes=VMEM_BYTES),
        name="mix_channels",
    )(order, near, far, gains, own_proj, other_proj, *so_far)


def add_tokens(order, tokens, pieces, sizes):
    _, rows, quarters, _ = sizes
    half = rows // 2

    def body(order, tokens_ref, *refs):
        out_ref = refs[-1]
        columns = pieces[0].shape[2]
        core = order[quarters + 2]
        for at_core in range(2):

            @pl.when(core == at_core)
            def _():
                for place in range(len(pieces)):
                    part, k = place // quarters, place % quarters
                    at = pl.ds(pl.multiple_of(order[k] * rows + part * half, half), half)
                    for side in range(2):
                        start = (at_core if side == 0 else 1 - at_core) * columns
                        across = slice(start, start + columns)
                        out_ref[at, across] = (
                            tokens_ref[at, across].astype(jnp.float32)
                            + refs[place][side].astype(jnp.float32)
                        ).astype(jnp.bfloat16)

    whole = lambda value: pl.BlockSpec(value.shape, lambda i, order: (0,) * value.ndim)
    return pl.pallas_call(
        body,
        out_shape=jax.ShapeDtypeStruct(tokens.shape, tokens.dtype),
        grid_spec=pltpu.PrefetchScalarGridSpec(
            num_scalar_prefetch=1,
            grid=(1,),
            in_specs=[whole(tokens)] + [whole(value) for value in pieces],
            out_specs=whole(tokens),
        ),
        compiler_params=pltpu.CompilerParams(vmem_limit_bytes=VMEM_BYTES),
        name="add_tokens",
    )(order, tokens, *pieces)


VALUE_GROUPS = ((0,), (1, 2, 3))


def by_channel(
    tokens,
    norm_gain,
    gate_proj,
    value_proj,
    step_proj,
    state_proj,
    conv_value,
    conv_state,
    step_bias,
    decay_rate,
    skip_gain,
    mix_gain,
    out_proj,
    doc_lengths,
):
    stretches = lax.axis_size("seq")
    quarters = lax.axis_size("fsdp")
    chips = stretches // 2
    span, features = tokens.shape
    rows = span // quarters
    depth, inner_width = gate_proj.shape
    width = inner_width // stretches
    head_count = step_bias.shape[0]
    heads = head_count // stretches
    total_tokens = stretches * span
    sizes = (stretches, rows, quarters, width)
    seq_index = lax.axis_index("seq")
    fsdp_index = lax.axis_index("fsdp")
    chip, core = seq_index // 2, seq_index % 2
    where = jnp.stack([chip, core])
    order = jnp.stack(
        [fsdp_index ^ k for k in range(quarters)]
        + [(seq_index * heads).astype(jnp.int32), chip, core]
    )

    state_cols = lax.dynamic_index_in_dim(state_proj, fsdp_index, 1, keepdims=False)
    small = jnp.concatenate(
        [state_cols, step_proj, jnp.zeros((depth, 128 - head_count), jnp.bfloat16)], axis=1
    )
    starts = jnp.cumsum(doc_lengths) - doc_lengths
    index = jnp.arange(total_tokens, dtype=jnp.int32)[:, None]
    ages = jnp.min(
        jnp.where(starts[None, :] <= index, index - starts[None, :], total_tokens),
        axis=1,
        keepdims=True,
    )
    own_part = lambda value: lax.dynamic_slice_in_dim(value, seq_index * heads, heads, 0)
    lanes = lambda value: jnp.pad(own_part(value), (0, 128 - heads))[None, :]
    bias, rate = lanes(step_bias), lanes(decay_rate)
    skip = jnp.repeat(own_part(skip_gain), HEAD_DIM)[None, :]
    taps = lax.dynamic_slice_in_dim(conv_value, seq_index * width, width, 1)
    state_taps = lax.dynamic_index_in_dim(conv_state, fsdp_index, 1, keepdims=False)

    other_proj = swap_cores(out_proj)
    parts = lax.all_to_all(
        tokens.reshape(quarters, rows, features), "fsdp", split_axis=0, concat_axis=0, tiled=True
    )
    as_float = parts.astype(jnp.float32)
    mean_square = jnp.sum(as_float * as_float, axis=(0, 2), keepdims=True) / (
        quarters * features
    )
    normed = (
        as_float * lax.rsqrt(mean_square + EPSILON) * norm_gain.reshape(quarters, 1, features)
    ).astype(jnp.bfloat16)
    slices = (
        normed.reshape(quarters, rows, stretches // quarters, depth)
        .transpose(0, 2, 1, 3)
        .reshape(stretches, rows, depth)
    )
    own = lax.all_to_all(slices, "seq", split_axis=0, concat_axis=0, tiled=True).reshape(
        stretches * rows, depth
    )
    own, small, ages, bias, rate, skip, taps, state_taps, order, where = lax.optimization_barrier(
        (own, small, ages, bias, rate, skip, taps, state_taps, order, where)
    )

    near = [flip_fsdp(own, 1), flip_fsdp(own, 2)]
    near[0], near[1], again = lax.optimization_barrier((near[0], near[1], own))
    pieces = [own, *near, flip_fsdp(again, 3)]

    def reduced(inputs, *weights):
        lent, kept = share_partials(inputs, *weights, where, chips, width)
        return ring_reduce(kept, lent)

    ahead, behind = VALUE_GROUPS
    later = [pieces[k] for k in behind]
    first = reduced([pieces[k] for k in ahead], value_proj, gate_proj, small)
    second = reduced(later, value_proj, None, small)
    third = reduced(later, gate_proj, None, None)
    thin = []
    for members, trio in zip(VALUE_GROUPS, (first, second)):
        begin = len(members) * stretches * rows
        end = begin + len(members) * (rows + rows // 2)
        thin.append(
            add_up(trio[0][0, begin:end], trio[1][0, begin:end], trio[2][begin:end]).astype(
                jnp.bfloat16
            )
        )
    thin = jnp.concatenate(thin, axis=0)
    spread = [thin]
    for away in range(1, chips):
        spread.append(next_chip(thin, away))
    thin = jnp.stack(spread)
    thin_swapped = swap_cores(thin)
    outputs = scan_heads(
        order, (first, second), VALUE_GROUPS, thin, thin_swapped, ages, taps, state_taps,
        bias, rate, skip, sizes,
    )
    gate_start = len(ahead) * (stretches * rows + rows + rows // 2)
    parts = gate_outputs(
        order, outputs, (first, third), VALUE_GROUPS, (gate_start, 0), sizes
    )
    gains = mix_gain.reshape(stretches, width)
    ended = []
    for part in range(2):
        flat = lambda value: value.reshape(total_tokens // 4, width)
        came = swap_cores(parts[2 + part])
        blocks = [jnp.stack([flat(parts[part]), flat(came)])]
        for _ in range(1, chips):
            blocks.append(next_chip(blocks[-1]))
        so_far = mix_channels(
            order, *blocks[:2], 0, None, gains, out_proj, other_proj, sizes
        )
        left_kept, left_sent, right_kept, right_sent = mix_channels(
            order, *blocks[2:], 2, so_far, gains, out_proj, other_proj, sizes
        )
        left_got = flip_fsdp(left_sent, 1)
        right_got = flip_fsdp(right_sent, 2)
        left_sum = add_up(left_kept[1], left_got[1]).astype(jnp.bfloat16)
        right_sum = add_up(right_kept[1], right_got[1]).astype(jnp.bfloat16)
        left_more = flip_fsdp(left_sum, 2)
        right_more = flip_fsdp(right_sum, 1)
        summed = jnp.stack(
            [
                add_up(left_kept[0], left_got[0], left_more).astype(jnp.bfloat16),
                add_up(right_kept[0], right_got[0], right_more).astype(jnp.bfloat16),
            ],
            axis=1,
        )
        to_chip = lambda away: lax.dynamic_index_in_dim(summed, (chip + away) % chips, 0, False)
        arrived = [to_chip(0)]
        for away in range(1, chips):
            arrived.append(next_chip(to_chip(away), away))
        arrived = jnp.stack(arrived)
        from_chip = lambda other: lax.dynamic_index_in_dim(
            arrived, (chip + chips - other) % chips, 0, False
        )
        ended.append(from_chip(fsdp_index))
        for k in range(1, quarters):
            ended.append(flip_fsdp(from_chip(fsdp_index ^ k), k))
    return add_tokens(order, tokens, ended, sizes)


def layer(*arguments):
    stretches, quarters = lax.axis_size("seq"), lax.axis_size("fsdp")
    span, inner_width = arguments[0].shape[0], arguments[2].shape[1]
    heads = arguments[8].shape[0]
    width = inner_width // stretches
    aligned = (
        quarters == G
        and quarters == 4
        and stretches == 2 * quarters
        and width == 2 * N
        and width % HEAD_DIM == 0
        and heads <= 128
        and span % (16 * quarters) == 0
        and span % 128 == 0
    )
    return (by_channel if aligned else by_stretch)(*arguments)


def solution(mesh):
    return jax.shard_map(
        layer,
        mesh=mesh,
        in_specs=(
            P("seq", "fsdp"),
            P(),
            P("seq", "fsdp"),
            P("seq", "fsdp"),
            P("seq", "fsdp"),
            P("seq", None, None),
            P(None, "fsdp"),
            P(),
            P("fsdp"),
            P("fsdp"),
            P("fsdp"),
            P("fsdp"),
            P("fsdp", "seq"),
            P(),
        ),
        out_specs=P("seq", "fsdp"),
        check_vma=False,
    )
```

profile of v0, /device:TPU:0, one launch (start us, length us, event | category | flops | bytes accessed | tf_op | source)
XLA Modules:
  0.0 282.8 jit_solution(991212013969345346)
XLA Ops:
  0.0 5.3 %all-to-all-start = ((bf16[4,32,2048]{2,1,0:T(8,128)(2,1)}), bf16[4,32,2048]{2,1,0:T(8,128)(2,1)S(1)}, u32[]{:S(2)}, u32[]{:S(2)}) async-start(bf16[4,32,2048]{2,1,0:T(8,128)(2,1)} %bitcast.149), calls=%async_computation | async-start | bytes 1048576 | tf_op jit(solution)/shard_map/all_to_all | solution.py:656
  9.0 4.3 %all-to-all-done = bf16[4,32,2048]{2,1,0:T(8,128)(2,1)S(1)} async-done(((bf16[4,32,2048]{2,1,0:T(8,128)(2,1)}), bf16[4,32,2048]{2,1,0:T(8,128)(2,1)S(1)}, u32[]{:S(2)}, u32[]{:S(2)}) %all-to-all-start) | async-done | bytes 524320 | tf_op jit(solution)/shard_map/all_to_all | solution.py:656
  14.7 4.9 %all-to-all-start.1 = ((bf16[8,32,1024]{2,1,0:T(8,128)(2,1)}), bf16[8,32,1024]{2,1,0:T(8,128)(2,1)S(1)}, u32[]{:S(2)}, u32[]{:S(2)}) async-start(bf16[8,32,1024]{2,1,0:T(8,128)(2,1)} %bitcast.1), calls=%async_computation.1 | async-start | bytes 1048576 | tf_op jit(solution)/shard_map/all_to_all | solution.py:671
  26.9 8.0 %all-to-all-done.1 = bf16[8,32,1024]{2,1,0:T(8,128)(2,1)S(1)} async-done(((bf16[8,32,1024]{2,1,0:T(8,128)(2,1)}), bf16[8,32,1024]{2,1,0:T(8,128)(2,1)S(1)}, u32[]{:S(2)}, u32[]{:S(2)}) %all-to-all-start.1) | async-done | bytes 524320 | tf_op jit(solution)/shard_map/all_to_all | solution.py:671
  36.9 11.4 %collective-permute-done.4.refs_0_ = bf16[256,1024]{1,0:T(8,128)(2,1)S(1)} collective-permute-done((bf16[256,1024]{1,0:T(8,128)(2,1)S(1)}, bf16[256,1024]{1,0:T(8,128)(2,1)S(1)}, u32[]{:S(2)}, u32[]{:S(2)}) %collective-permute-start.4) | collective-permute-done | bytes 524320 | tf_op jit(solution)/shard_map/ppermute | solution.py:171
  50.9 11.6 %collective-permute-done.6.refs_2_ = bf16[256,1024]{1,0:T(8,128)(2,1)S(1)} collective-permute-done((bf16[256,1024]{1,0:T(8,128)(2,1)S(1)}, bf16[256,1024]{1,0:T(8,128)(2,1)S(1)}, u32[]{:S(2)}, u32[]{:S(2)}) %collective-permute-start.6) | collective-permute-done | bytes 524320 | tf_op jit(solution)/shard_map/ppermute | solution.py:171
  63.4 9.2 %share_partials.5 = (bf16[4,912,256]{2,1,0:T(8,128)(2,1)}, bf16[4,912,256]{2,1,0:T(8,128)(2,1)}) custom-call(s32[2]{0:T(128)} %pad_add_fusion.where, bf16[256,1024]{1,0:T(8,128)(2,1)} %copy-done.7, bf16[256,1024]{1,0:T(8,128)(2,1)} %copy-done.8, bf16[256,1024]{1,0:T(8,128)(2,1)} %copy-done.9, bf16[1024,2048]{1,0:T(8,128)(2,1)} %refs_3_.3, ...), custom_call_target="tpu_custom_call" | custom-call | tf_op jit(solution)/shard_map/share_partials/pallas_call | solution.py:230
  72.6 8.1 %share_partials.3 = (bf16[4,560,256]{2,1,0:T(8,128)(2,1)}, bf16[4,560,256]{2,1,0:T(8,128)(2,1)}) custom-call(s32[2]{0:T(128)} %pad_add_fusion.where, bf16[256,1024]{1,0:T(8,128)(2,1)} %bitcast.148, bf16[1024,2048]{1,0:T(8,128)(2,1)} %refs_3_.3, bf16[1024,2048]{1,0:T(8,128)(2,1)} %refs_3_.2, bf16[1024,384]{1,0:T(8,128)(2,1)} %maximum_maximum_fusion.refs_3_.refs_4_), custom_call_target="tpu_custom_call" | custom-call | tf_op jit(solution)/shard_map/share_partials/pallas_call | solution.py:230
  81.2 8.0 %share_partials.4 = (bf16[4,768,256]{2,1,0:T(8,128)(2,1)}, bf16[4,768,256]{2,1,0:T(8,128)(2,1)}) custom-call(s32[2]{0:T(128)} %pad_add_fusion.where, bf16[256,1024]{1,0:T(8,128)(2,1)} %copy-done.7, bf16[256,1024]{1,0:T(8,128)(2,1)} %copy-done.8, bf16[256,1024]{1,0:T(8,128)(2,1)} %copy-done.9, bf16[1024,2048]{1,0:T(8,128)(2,1)} %refs_3_.2), custom_call_target="tpu_custom_call" | custom-call | tf_op jit(solution)/shard_map/share_partials/pallas_call | solution.py:230
  91.4 9.5 %collective-permute-done.1 = bf16[560,256]{1,0:T(8,128)(2,1)S(1)} collective-permute-done((bf16[560,256]{1,0:T(8,128)(2,1)S(1)}, bf16[560,256]{1,0:T(8,128)(2,1)S(1)}, u32[]{:S(2)}, u32[]{:S(2)}) %collective-permute-start.1) | collective-permute-done | bytes 286752 | tf_op jit(solution)/shard_map/ppermute | solution.py:166
  101.1 9.8 %collective-permute-done.12 = bf16[912,256]{1,0:T(8,128)(2,1)S(1)} collective-permute-done((bf16[912,256]{1,0:T(8,128)(2,1)S(1)}, bf16[912,256]{1,0:T(8,128)(2,1)S(1)}, u32[]{:S(2)}, u32[]{:S(2)}) %collective-permute-start.12) | collective-permute-done | bytes 466976 | tf_op jit(solution)/shard_map/ppermute | solution.py:166
  112.2 4.9 %collective-permute-done.2 = bf16[560,256]{1,0:T(8,128)(2,1)S(1)} collective-permute-done((bf16[560,256]{1,0:T(8,128)(2,1)S(1)}, bf16[560,256]{1,0:T(8,128)(2,1)S(1)}, u32[]{:S(2)}, u32[]{:S(2)}) %collective-permute-start.2) | collective-permute-done | bytes 286752 | tf_op jit(solution)/shard_map/ppermute | solution.py:166
  117.5 10.1 %collective-permute-done.13 = bf16[912,256]{1,0:T(8,128)(2,1)S(1)} collective-permute-done((bf16[912,256]{1,0:T(8,128)(2,1)S(1)}, bf16[912,256]{1,0:T(8,128)(2,1)S(1)}, u32[]{:S(2)}, u32[]{:S(2)}) %collective-permute-start.13) | collective-permute-done | bytes 466976 | tf_op jit(solution)/shard_map/ppermute | solution.py:166
  128.8 4.9 %collective-permute-done.3.refs_2_ = bf16[560,256]{1,0:T(8,128)(2,1)S(1)} collective-permute-done((bf16[560,256]{1,0:T(8,128)(2,1)S(1)}, bf16[560,256]{1,0:T(8,128)(2,1)S(1)}, u32[]{:S(2)}, u32[]{:S(2)}) %collective-permute-start.3) | collective-permute-done | bytes 286752 | tf_op jit(solution)/shard_map/ppermute | solution.py:166
  133.7 8.4 %collective-permute-done.8 = bf16[768,256]{1,0:T(8,128)(2,1)S(1)} collective-permute-done((bf16[768,256]{1,0:T(8,128)(2,1)S(1)}, bf16[768,256]{1,0:T(8,128)(2,1)S(1)}, u32[]{:S(2)}, u32[]{:S(2)}) %collective-permute-start.8) | collective-permute-done | bytes 393248 | tf_op jit(solution)/shard_map/ppermute | solution.py:166
  142.3 9.8 %collective-permute-done.14.refs_5_ = bf16[912,256]{1,0:T(8,128)(2,1)S(1)} collective-permute-done((bf16[912,256]{1,0:T(8,128)(2,1)S(1)}, bf16[912,256]{1,0:T(8,128)(2,1)S(1)}, u32[]{:S(2)}, u32[]{:S(2)}) %collective-permute-start.14) | collective-permute-done | bytes 466976 | tf_op jit(solution)/shard_map/ppermute | solution.py:166
  153.8 3.2 %collective-permute-start.17 = (bf16[192,256]{1,0:T(8,128)(2,1)S(1)}, bf16[192,256]{1,0:T(8,128)(2,1)S(1)}, u32[]{:S(2)}, u32[]{:S(2)}) collective-permute-start(bf16[192,256]{1,0:T(8,128)(2,1)S(1)} %get-tuple-element.94), channel_id=1, source_target_pairs={{0,24},{4,28},{8,0},{12,4},{16,8},{20,12},{24,16},{28,20},{1,25},{... | collective-permute-start | bytes 294920 | tf_op jit(solution)/shard_map/ppermute | solution.py:166
  157.0 5.8 %collective-permute-done.15 = bf16[192,256]{1,0:T(8,128)(2,1)S(1)} collective-permute-done((bf16[192,256]{1,0:T(8,128)(2,1)S(1)}, bf16[192,256]{1,0:T(8,128)(2,1)S(1)}, u32[]{:S(2)}, u32[]{:S(2)}) %collective-permute-start.15) | collective-permute-done | bytes 98336 | tf_op jit(solution)/shard_map/ppermute | solution.py:166
  162.8 3.3 %collective-permute-done.16 = bf16[192,256]{1,0:T(8,128)(2,1)S(1)} collective-permute-done((bf16[192,256]{1,0:T(8,128)(2,1)S(1)}, bf16[192,256]{1,0:T(8,128)(2,1)S(1)}, u32[]{:S(2)}, u32[]{:S(2)}) %collective-permute-start.16) | collective-permute-done | bytes 98336 | tf_op jit(solution)/shard_map/ppermute | solution.py:166
  170.7 11.7 %scan_heads.1 = f32[1024,256]{1,0:T(8,128)} custom-call(s32[7]{0:T(128)} %stack.101.order, bf16[4,560,256]{2,1,0:T(8,128)(2,1)} %get-tuple-element.44.refs_0_, bf16[4,560,256]{2,1,0:T(8,128)(2,1)} %copy-done.2, bf16[560,256]{1,0:T(8,128)(2,1)} %copy-done.11, bf16[4,912,256]{2,1,0:T(8,128)(2,1)} %get-tuple-element.51.refs_3_, ...), custom_call_target="tpu_custom_call" | custom-call | tf_op jit(solution)/shard_map/scan_heads/pallas_call | solution.py:407
  182.4 3.8 %gate_outputs.1 = (bf16[4,4,16,256]{3,2,1,0:T(8,128)(2,1)}, bf16[4,4,16,256]{3,2,1,0:T(8,128)(2,1)}, bf16[4,4,16,256]{3,2,1,0:T(8,128)(2,1)}, bf16[4,4,16,256]{3,2,1,0:T(8,128)(2,1)}) custom-call(s32[7]{0:T(128)} %stack.101.order, bf16[4,560,256]{2,1,0:T(8,128)(2,1)} %get-tuple-element.44.refs_0_, bf16[4,560,256]{2,1,0:T(8,128)(2,1)} %copy-done.2, ...), custom_call_target="tpu_custom_call" | custom-call | tf_op jit(solution)/shard_map/gate_outputs/pallas_call | solution.py:462
  191.5 8.2 %collective-permute-done.35.far_ref = bf16[2,256,256]{2,1,0:T(8,128)(2,1)S(1)} collective-permute-done((bf16[2,256,256]{2,1,0:T(8,128)(2,1)S(1)}, bf16[2,256,256]{2,1,0:T(8,128)(2,1)S(1)}, u32[]{:S(2)}, u32[]{:S(2)}) %collective-permute-start.35) | collective-permute-done | bytes 262176 | tf_op jit(solution)/shard_map/ppermute | solution.py:166
  199.7 5.6 %collective-permute-done.20.far_ref = bf16[2,256,256]{2,1,0:T(8,128)(2,1)S(1)} collective-permute-done((bf16[2,256,256]{2,1,0:T(8,128)(2,1)S(1)}, bf16[2,256,256]{2,1,0:T(8,128)(2,1)S(1)}, u32[]{:S(2)}, u32[]{:S(2)}) %collective-permute-start.20) | collective-permute-done | bytes 262176 | tf_op jit(solution)/shard_map/ppermute | solution.py:166
  205.3 5.6 %collective-permute-done.36.near_ref = bf16[2,256,256]{2,1,0:T(8,128)(2,1)S(1)} collective-permute-done((bf16[2,256,256]{2,1,0:T(8,128)(2,1)S(1)}, bf16[2,256,256]{2,1,0:T(8,128)(2,1)S(1)}, u32[]{:S(2)}, u32[]{:S(2)}) %collective-permute-start.36) | collective-permute-done | bytes 262176 | tf_op jit(solution)/shard_map/ppermute | solution.py:166
  211.6 4.9 %collective-permute-done.21.near_ref = bf16[2,256,256]{2,1,0:T(8,128)(2,1)S(1)} collective-permute-done((bf16[2,256,256]{2,1,0:T(8,128)(2,1)S(1)}, bf16[2,256,256]{2,1,0:T(8,128)(2,1)S(1)}, u32[]{:S(2)}, u32[]{:S(2)}) %collective-permute-start.21) | collective-permute-done | bytes 262176 | tf_op jit(solution)/shard_map/ppermute | solution.py:166
  216.6 6.2 %mix_channels.6 = (f32[256,2048]{1,0:T(8,128)}, f32[256,128]{1,0:T(8,128)}) custom-call(s32[7]{0:T(128)} %stack.101.order, bf16[2,256,256]{2,1,0:T(8,128)(2,1)} %copy-done.13, bf16[2,256,256]{2,1,0:T(8,128)(2,1)} %copy-done.23, f32[8,256]{1,0:T(8,128)} %reshape.123.gains_ref, bf16[2048,1024]{1,0:T(8,128)(2,1)} %own_ref.7, ...), custom_call_target="tpu_custom_call" | custom-call | tf_op jit(solution)/shard_map/mix_channels/pallas_call | solution.py:538
  222.9 7.0 %mix_channels.7 = (bf16[2,4,16,1024]{3,2,1,0:T(8,128)(2,1)}, bf16[2,4,16,1024]{3,2,1,0:T(8,128)(2,1)}, bf16[2,4,16,1024]{3,2,1,0:T(8,128)(2,1)}, bf16[2,4,16,1024]{3,2,1,0:T(8,128)(2,1)}) custom-call(s32[7]{0:T(128)} %stack.101.order, bf16[2,256,256]{2,1,0:T(8,128)(2,1)} %copy-done.17, bf16[2,256,256]{2,1,0:T(8,128)(2,1)} %collective-permute-done.37.far_ref, ...), custom_call_target="tpu_custom_call" | custom-call | tf_op jit(solution)/shard_map/mix_channels/pallas_call | solution.py:538
  231.9 6.2 %mix_channels.4 = (f32[256,2048]{1,0:T(8,128)}, f32[256,128]{1,0:T(8,128)}) custom-call(s32[7]{0:T(128)} %stack.101.order, bf16[2,256,256]{2,1,0:T(8,128)(2,1)} %copy-done.12, bf16[2,256,256]{2,1,0:T(8,128)(2,1)} %copy-done.22, f32[8,256]{1,0:T(8,128)} %reshape.123.gains_ref, bf16[2048,1024]{1,0:T(8,128)(2,1)} %own_ref.7, ...), custom_call_target="tpu_custom_call" | custom-call | tf_op jit(solution)/shard_map/mix_channels/pallas_call | solution.py:538
  238.9 7.1 %mix_channels.5 = (bf16[2,4,16,1024]{3,2,1,0:T(8,128)(2,1)}, bf16[2,4,16,1024]{3,2,1,0:T(8,128)(2,1)}, bf16[2,4,16,1024]{3,2,1,0:T(8,128)(2,1)}, bf16[2,4,16,1024]{3,2,1,0:T(8,128)(2,1)}) custom-call(s32[7]{0:T(128)} %stack.101.order, bf16[2,256,256]{2,1,0:T(8,128)(2,1)} %copy-done.15, bf16[2,256,256]{2,1,0:T(8,128)(2,1)} %copy-done.16, ...), custom_call_target="tpu_custom_call" | custom-call | tf_op jit(solution)/shard_map/mix_channels/pallas_call | solution.py:538
  250.2 3.6 %collective-permute-done.26 = bf16[2,4,16,1024]{3,2,1,0:T(8,128)(2,1)S(1)} collective-permute-done((bf16[2,4,16,1024]{3,2,1,0:T(8,128)(2,1)}, bf16[2,4,16,1024]{3,2,1,0:T(8,128)(2,1)S(1)}, u32[]{:S(2)}, u32[]{:S(2)}) %collective-permute-start.26) | collective-permute-done | bytes 262176 | tf_op jit(solution)/shard_map/ppermute | solution.py:171
  258.2 4.1 %collective-permute-start.43 = (bf16[2,16,1024]{2,1,0:T(8,128)(2,1)S(1)}, bf16[2,16,1024]{2,1,0:T(8,128)(2,1)S(1)}, u32[]{:S(2)}, u32[]{:S(2)}) collective-permute-start(bf16[2,16,1024]{2,1,0:T(8,128)(2,1)S(1)} %get-tuple-element.83), channel_id=1, source_target_pairs={{0,16},{4,20},{8,24},{12,28},{16,0},{20,4},{24,8},{28,12},{1,17},{... | collective-permute-start | bytes 196616 | tf_op jit(solution)/shard_map/ppermute | solution.py:166
  280.1 2.8 add_tokens.1
  (203 shorter events, 65.1 us)
Async XLA Ops:
  0.0 13.3 %all-to-all-start = ((bf16[4,32,2048]{2,1,0:T(8,128)(2,1)}), bf16[4,32,2048]{2,1,0:T(8,128)(2,1)S(1)}, u32[]{:S(2)}, u32[]{:S(2)}) async-start(bf16[4,32,2048]{2,1,0:T(8,128)(2,1)} %bitcast.149), calls=%async_computation | async-start | bytes 1048576 | tf_op jit(solution)/shard_map/all_to_all | solution.py:656
  14.7 20.2 %all-to-all-start.1 = ((bf16[8,32,1024]{2,1,0:T(8,128)(2,1)}), bf16[8,32,1024]{2,1,0:T(8,128)(2,1)S(1)}, u32[]{:S(2)}, u32[]{:S(2)}) async-start(bf16[8,32,1024]{2,1,0:T(8,128)(2,1)} %bitcast.1), calls=%async_computation.1 | async-start | bytes 1048576 | tf_op jit(solution)/shard_map/all_to_all | solution.py:671
  34.9 13.4 %collective-permute-start.4 = (bf16[256,1024]{1,0:T(8,128)(2,1)S(1)}, bf16[256,1024]{1,0:T(8,128)(2,1)S(1)}, u32[]{:S(2)}, u32[]{:S(2)}) collective-permute-start(bf16[256,1024]{1,0:T(8,128)(2,1)S(1)} %bitcast.145), channel_id=1, source_target_pairs={{0,1},{1,0},{2,3},{3,2},{4,5},{5,4},{6,7},{7,6},{8,9},{9,8},{10,11... | collective-permute-start | bytes 1572872 | tf_op jit(solution)/shard_map/ppermute | solution.py:171
  36.3 13.1 %collective-permute-start.5 = (bf16[256,1024]{1,0:T(8,128)(2,1)S(1)}, bf16[256,1024]{1,0:T(8,128)(2,1)S(1)}, u32[]{:S(2)}, u32[]{:S(2)}) collective-permute-start(bf16[256,1024]{1,0:T(8,128)(2,1)S(1)} %bitcast.146), channel_id=1, source_target_pairs={{0,2},{1,3},{2,0},{3,1},{4,6},{5,7},{6,4},{7,5},{8,10},{9,11},{10,... | collective-permute-start | bytes 1572872 | tf_op jit(solution)/shard_map/ppermute | solution.py:171
  49.4 13.1 %collective-permute-start.6 = (bf16[256,1024]{1,0:T(8,128)(2,1)S(1)}, bf16[256,1024]{1,0:T(8,128)(2,1)S(1)}, u32[]{:S(2)}, u32[]{:S(2)}) collective-permute-start(bf16[256,1024]{1,0:T(8,128)(2,1)S(1)} %bitcast.147), channel_id=1, source_target_pairs={{0,3},{1,2},{2,1},{3,0},{4,7},{5,6},{6,5},{7,4},{8,11},{9,10},{10,... | collective-permute-start | bytes 1572872 | tf_op jit(solution)/shard_map/ppermute | solution.py:171
  72.6 16.9 %collective-permute-start.11 = (bf16[4,912,256]{2,1,0:T(8,128)(2,1)}, bf16[4,912,256]{2,1,0:T(8,128)(2,1)}, u32[]{:S(2)}, u32[]{:S(2)}) collective-permute-start(bf16[4,912,256]{2,1,0:T(8,128)(2,1)} %get-tuple-element.52), channel_id=1, source_target_pairs={{0,4},{4,0},{8,12},{12,8},{16,20},{20,16},{24,28},{28,24},{1,5},{5... | collective-permute-start | bytes 5603336 | tf_op jit(solution)/shard_map/ppermute | solution.py:160
  89.2 28.0 %collective-permute-start.7 = (bf16[4,768,256]{2,1,0:T(8,128)(2,1)}, bf16[4,768,256]{2,1,0:T(8,128)(2,1)S(1)}, u32[]{:S(2)}, u32[]{:S(2)}) collective-permute-start(bf16[4,768,256]{2,1,0:T(8,128)(2,1)} %get-tuple-element.50), channel_id=1, source_target_pairs={{0,4},{4,0},{8,12},{12,8},{16,20},{20,16},{24,28},{28,24},{1,5},{5... | collective-permute-start | bytes 4718600 | tf_op jit(solution)/shard_map/ppermute | solution.py:160
  89.3 11.6 %collective-permute-start.1 = (bf16[560,256]{1,0:T(8,128)(2,1)S(1)}, bf16[560,256]{1,0:T(8,128)(2,1)S(1)}, u32[]{:S(2)}, u32[]{:S(2)}) collective-permute-start(bf16[560,256]{1,0:T(8,128)(2,1)S(1)} %fusion.11), channel_id=1, source_target_pairs={{0,8},{4,12},{8,16},{12,20},{16,24},{20,28},{24,0},{28,4},{1,9},{5... | collective-permute-start | bytes 860168 | tf_op jit(solution)/shard_map/ppermute | solution.py:166
  90.8 20.1 %collective-permute-start.12 = (bf16[912,256]{1,0:T(8,128)(2,1)S(1)}, bf16[912,256]{1,0:T(8,128)(2,1)S(1)}, u32[]{:S(2)}, u32[]{:S(2)}) collective-permute-start(bf16[912,256]{1,0:T(8,128)(2,1)S(1)} %fusion.9), channel_id=1, source_target_pairs={{0,8},{4,12},{8,16},{12,20},{16,24},{20,28},{24,0},{28,4},{1,9},{5... | collective-permute-start | bytes 1400840 | tf_op jit(solution)/shard_map/ppermute | solution.py:166
  90.9 125.7 %collective-permute-start.23 = (bf16[2048,1024]{1,0:T(8,128)(2,1)}, bf16[2048,1024]{1,0:T(8,128)(2,1)}, u32[]{:S(2)}, u32[]{:S(2)}) collective-permute-start(bf16[2048,1024]{1,0:T(8,128)(2,1)} %own_ref.7), channel_id=1, source_target_pairs={{0,4},{4,0},{8,12},{12,8},{16,20},{20,16},{24,28},{28,24},{1,5},{5... | collective-permute-start | bytes 12582920 | tf_op jit(solution)/shard_map/ppermute | solution.py:160
  101.0 16.0 %collective-permute-start.2 = (bf16[560,256]{1,0:T(8,128)(2,1)S(1)}, bf16[560,256]{1,0:T(8,128)(2,1)S(1)}, u32[]{:S(2)}, u32[]{:S(2)}) collective-permute-start(bf16[560,256]{1,0:T(8,128)(2,1)S(1)} %fusion.7), channel_id=1, source_target_pairs={{0,8},{4,12},{8,16},{12,20},{16,24},{20,28},{24,0},{28,4},{1,9},{5... | collective-permute-start | bytes 860168 | tf_op jit(solution)/shard_map/ppermute | solution.py:166
  112.1 15.4 %collective-permute-start.13 = (bf16[912,256]{1,0:T(8,128)(2,1)S(1)}, bf16[912,256]{1,0:T(8,128)(2,1)S(1)}, u32[]{:S(2)}, u32[]{:S(2)}) collective-permute-start(bf16[912,256]{1,0:T(8,128)(2,1)S(1)} %fusion.3), channel_id=1, source_target_pairs={{0,8},{4,12},{8,16},{12,20},{16,24},{20,28},{24,0},{28,4},{1,9},{5... | collective-permute-start | bytes 1400840 | tf_op jit(solution)/shard_map/ppermute | solution.py:166
  117.2 16.5 %collective-permute-start.3 = (bf16[560,256]{1,0:T(8,128)(2,1)S(1)}, bf16[560,256]{1,0:T(8,128)(2,1)S(1)}, u32[]{:S(2)}, u32[]{:S(2)}) collective-permute-start(bf16[560,256]{1,0:T(8,128)(2,1)S(1)} %fusion.8), channel_id=1, source_target_pairs={{0,8},{4,12},{8,16},{12,20},{16,24},{20,28},{24,0},{28,4},{1,9},{5... | collective-permute-start | bytes 860168 | tf_op jit(solution)/shard_map/ppermute | solution.py:166
  117.4 24.7 %collective-permute-start.8 = (bf16[768,256]{1,0:T(8,128)(2,1)S(1)}, bf16[768,256]{1,0:T(8,128)(2,1)S(1)}, u32[]{:S(2)}, u32[]{:S(2)}) collective-permute-start(bf16[768,256]{1,0:T(8,128)(2,1)S(1)} %fusion.10), channel_id=1, source_target_pairs={{0,8},{4,12},{8,16},{12,20},{16,24},{20,28},{24,0},{28,4},{1,9},{5... | collective-permute-start | bytes 1179656 | tf_op jit(solution)/shard_map/ppermute | solution.py:166
  128.7 23.4 %collective-permute-start.14 = (bf16[912,256]{1,0:T(8,128)(2,1)S(1)}, bf16[912,256]{1,0:T(8,128)(2,1)S(1)}, u32[]{:S(2)}, u32[]{:S(2)}) collective-permute-start(bf16[912,256]{1,0:T(8,128)(2,1)S(1)} %fusion.4), channel_id=1, source_target_pairs={{0,8},{4,12},{8,16},{12,20},{16,24},{20,28},{24,0},{28,4},{1,9},{5... | collective-permute-start | bytes 1400840 | tf_op jit(solution)/shard_map/ppermute | solution.py:166
  142.2 23.9 %collective-permute-start.9 = (bf16[768,256]{1,0:T(8,128)(2,1)S(1)}, bf16[768,256]{1,0:T(8,128)(2,1)S(1)}, u32[]{:S(2)}, u32[]{:S(2)}) collective-permute-start(bf16[768,256]{1,0:T(8,128)(2,1)S(1)} %fusion.5), channel_id=1, source_target_pairs={{0,8},{4,12},{8,16},{12,20},{16,24},{20,28},{24,0},{28,4},{1,9},{5... | collective-permute-start | bytes 1179656 | tf_op jit(solution)/shard_map/ppermute | solution.py:166
  153.1 9.7 %collective-permute-start.15 = (bf16[192,256]{1,0:T(8,128)(2,1)S(1)}, bf16[192,256]{1,0:T(8,128)(2,1)S(1)}, u32[]{:S(2)}, u32[]{:S(2)}) collective-permute-start(bf16[192,256]{1,0:T(8,128)(2,1)S(1)} %get-tuple-element.94), channel_id=1, source_target_pairs={{0,8},{4,12},{8,16},{12,20},{16,24},{20,28},{24,0},{28,4},{1,9},{5... | collective-permute-start | bytes 294920 | tf_op jit(solution)/shard_map/ppermute | solution.py:166
  153.2 12.9 %collective-permute-start.16 = (bf16[192,256]{1,0:T(8,128)(2,1)S(1)}, bf16[192,256]{1,0:T(8,128)(2,1)S(1)}, u32[]{:S(2)}, u32[]{:S(2)}) collective-permute-start(bf16[192,256]{1,0:T(8,128)(2,1)S(1)} %get-tuple-element.94), channel_id=1, source_target_pairs={{0,16},{4,20},{8,24},{12,28},{16,0},{20,4},{24,8},{28,12},{1,17},{... | collective-permute-start | bytes 294920 | tf_op jit(solution)/shard_map/ppermute | solution.py:166
  153.8 12.3 %collective-permute-start.17 = (bf16[192,256]{1,0:T(8,128)(2,1)S(1)}, bf16[192,256]{1,0:T(8,128)(2,1)S(1)}, u32[]{:S(2)}, u32[]{:S(2)}) collective-permute-start(bf16[192,256]{1,0:T(8,128)(2,1)S(1)} %get-tuple-element.94), channel_id=1, source_target_pairs={{0,24},{4,28},{8,0},{12,4},{16,8},{20,12},{24,16},{28,20},{1,25},{... | collective-permute-start | bytes 294920 | tf_op jit(solution)/shard_map/ppermute | solution.py:166
  167.1 15.3 %collective-permute-start.10 = (bf16[768,256]{1,0:T(8,128)(2,1)}, bf16[768,256]{1,0:T(8,128)(2,1)}, u32[]{:S(2)}, u32[]{:S(2)}) collective-permute-start(bf16[768,256]{1,0:T(8,128)(2,1)} %fusion.6), channel_id=1, source_target_pairs={{0,8},{4,12},{8,16},{12,20},{16,24},{20,28},{24,0},{28,4},{1,9},{5... | collective-permute-start | bytes 1179656 | tf_op jit(solution)/shard_map/ppermute | solution.py:166
  188.7 11.0 %collective-permute-start.35 = (bf16[2,256,256]{2,1,0:T(8,128)(2,1)S(1)}, bf16[2,256,256]{2,1,0:T(8,128)(2,1)S(1)}, u32[]{:S(2)}, u32[]{:S(2)}) collective-permute-start(bf16[2,256,256]{2,1,0:T(8,128)(2,1)S(1)} %pad_maximum_fusion.4.near_ref), channel_id=1, source_target_pairs={{0,8},{4,12},{8,16},{12,20},{16,24},{20,28},{24,0},{28,4},{1,9},{5... | collective-permute-start | bytes 786440 | tf_op jit(solution)/shard_map/ppermute | solution.py:166
  191.4 14.0 %collective-permute-start.20 = (bf16[2,256,256]{2,1,0:T(8,128)(2,1)S(1)}, bf16[2,256,256]{2,1,0:T(8,128)(2,1)S(1)}, u32[]{:S(2)}, u32[]{:S(2)}) collective-permute-start(bf16[2,256,256]{2,1,0:T(8,128)(2,1)S(1)} %pad_maximum_fusion.2.near_ref), channel_id=1, source_target_pairs={{0,8},{4,12},{8,16},{12,20},{16,24},{20,28},{24,0},{28,4},{1,9},{5... | collective-permute-start | bytes 786440 | tf_op jit(solution)/shard_map/ppermute | solution.py:166
  199.7 11.2 %collective-permute-start.36 = (bf16[2,256,256]{2,1,0:T(8,128)(2,1)S(1)}, bf16[2,256,256]{2,1,0:T(8,128)(2,1)S(1)}, u32[]{:S(2)}, u32[]{:S(2)}) collective-permute-start(bf16[2,256,256]{2,1,0:T(8,128)(2,1)S(1)} %collective-permute-done.35.far_ref), channel_id=1, source_target_pairs={{0,8},{4,12},{8,16},{12,20},{16,24},{20,28},{24,0},{28,4},{1,9},{5... | collective-permute-start | bytes 786440 | tf_op jit(solution)/shard_map/ppermute | solution.py:166
  205.3 11.2 %collective-permute-start.21 = (bf16[2,256,256]{2,1,0:T(8,128)(2,1)S(1)}, bf16[2,256,256]{2,1,0:T(8,128)(2,1)S(1)}, u32[]{:S(2)}, u32[]{:S(2)}) collective-permute-start(bf16[2,256,256]{2,1,0:T(8,128)(2,1)S(1)} %collective-permute-done.20.far_ref), channel_id=1, source_target_pairs={{0,8},{4,12},{8,16},{12,20},{16,24},{20,28},{24,0},{28,4},{1,9},{5... | collective-permute-start | bytes 786440 | tf_op jit(solution)/shard_map/ppermute | solution.py:166
  211.0 11.9 %collective-permute-start.37 = (bf16[2,256,256]{2,1,0:T(8,128)(2,1)S(1)}, bf16[2,256,256]{2,1,0:T(8,128)(2,1)}, u32[]{:S(2)}, u32[]{:S(2)}) collective-permute-start(bf16[2,256,256]{2,1,0:T(8,128)(2,1)S(1)} %collective-permute-done.36.near_ref), channel_id=1, source_target_pairs={{0,8},{4,12},{8,16},{12,20},{16,24},{20,28},{24,0},{28,4},{1,9},{5... | collective-permute-start | bytes 786440 | tf_op jit(solution)/shard_map/ppermute | solution.py:166
  216.6 21.6 %collective-permute-start.22 = (bf16[2,256,256]{2,1,0:T(8,128)(2,1)S(1)}, bf16[2,256,256]{2,1,0:T(8,128)(2,1)S(1)}, u32[]{:S(2)}, u32[]{:S(2)}) collective-permute-start(bf16[2,256,256]{2,1,0:T(8,128)(2,1)S(1)} %collective-permute-done.21.near_ref), channel_id=1, source_target_pairs={{0,8},{4,12},{8,16},{12,20},{16,24},{20,28},{24,0},{28,4},{1,9},{5... | collective-permute-start | bytes 786440 | tf_op jit(solution)/shard_map/ppermute | solution.py:166
  229.8 18.1 %collective-permute-start.40 = (bf16[2,4,16,1024]{3,2,1,0:T(8,128)(2,1)}, bf16[2,4,16,1024]{3,2,1,0:T(8,128)(2,1)S(1)}, u32[]{:S(2)}, u32[]{:S(2)}) collective-permute-start(bf16[2,4,16,1024]{3,2,1,0:T(8,128)(2,1)} %get-tuple-element.74), channel_id=1, source_target_pairs={{0,2},{1,3},{2,0},{3,1},{4,6},{5,7},{6,4},{7,5},{8,10},{9,11},{10,... | collective-permute-start | bytes 786440 | tf_op jit(solution)/shard_map/ppermute | solution.py:171
  230.5 18.2 %collective-permute-start.38 = (bf16[2,4,16,1024]{3,2,1,0:T(8,128)(2,1)}, bf16[2,4,16,1024]{3,2,1,0:T(8,128)(2,1)S(1)}, u32[]{:S(2)}, u32[]{:S(2)}) collective-permute-start(bf16[2,4,16,1024]{3,2,1,0:T(8,128)(2,1)} %get-tuple-element.72), channel_id=1, source_target_pairs={{0,1},{1,0},{2,3},{3,2},{4,5},{5,4},{6,7},{7,6},{8,9},{9,8},{10,11... | collective-permute-start | bytes 786440 | tf_op jit(solution)/shard_map/ppermute | solution.py:171
  246.5 8.9 %collective-permute-start.24 = (bf16[2,4,16,1024]{3,2,1,0:T(8,128)(2,1)}, bf16[2,4,16,1024]{3,2,1,0:T(8,128)(2,1)S(1)}, u32[]{:S(2)}, u32[]{:S(2)}) collective-permute-start(bf16[2,4,16,1024]{3,2,1,0:T(8,128)(2,1)} %get-tuple-element.64), channel_id=1, source_target_pairs={{0,1},{1,0},{2,3},{3,2},{4,5},{5,4},{6,7},{7,6},{8,9},{9,8},{10,11... | collective-permute-start | bytes 786440 | tf_op jit(solution)/shard_map/ppermute | solution.py:171
  248.0 10.0 %collective-permute-start.41 = (bf16[4,16,1024]{2,1,0:T(8,128)(2,1)S(1)}, bf16[4,16,1024]{2,1,0:T(8,128)(2,1)S(1)}, u32[]{:S(2)}, u32[]{:S(2)}) collective-permute-start(bf16[4,16,1024]{2,1,0:T(8,128)(2,1)S(1)} %fusion.20), channel_id=1, source_target_pairs={{0,1},{1,0},{2,3},{3,2},{4,5},{5,4},{6,7},{7,6},{8,9},{9,8},{10,11... | collective-permute-start | bytes 393224 | tf_op jit(solution)/shard_map/ppermute | solution.py:171
  248.7 9.3 %collective-permute-start.39 = (bf16[4,16,1024]{2,1,0:T(8,128)(2,1)S(1)}, bf16[4,16,1024]{2,1,0:T(8,128)(2,1)S(1)}, u32[]{:S(2)}, u32[]{:S(2)}) collective-permute-start(bf16[4,16,1024]{2,1,0:T(8,128)(2,1)S(1)} %fusion.19), channel_id=1, source_target_pairs={{0,2},{1,3},{2,0},{3,1},{4,6},{5,7},{6,4},{7,5},{8,10},{9,11},{10,... | collective-permute-start | bytes 393224 | tf_op jit(solution)/shard_map/ppermute | solution.py:171
  258.2 9.2 %collective-permute-start.43 = (bf16[2,16,1024]{2,1,0:T(8,128)(2,1)S(1)}, bf16[2,16,1024]{2,1,0:T(8,128)(2,1)S(1)}, u32[]{:S(2)}, u32[]{:S(2)}) collective-permute-start(bf16[2,16,1024]{2,1,0:T(8,128)(2,1)S(1)} %get-tuple-element.83), channel_id=1, source_target_pairs={{0,16},{4,20},{8,24},{12,28},{16,0},{20,4},{24,8},{28,12},{1,17},{... | collective-permute-start | bytes 196616 | tf_op jit(solution)/shard_map/ppermute | solution.py:166
  (51 other events, 566.7 us)
where the time goes:
time: 284 us; the launch traced here: 283 us
  waiting for transfers between devices  137 us (48%)
  Pallas kernels  70.1 us (25%)
  starting transfers between devices  47 us (17%)
  local copies, waits for them, and re-layouts  14.2 us (5%)
  other arithmetic  13.7 us (5%)
    ppermute x24, waiting for transfers between devices, next_chip(): return lax.ppermute(value, 'seq', route)  90.7 us
    ppermute x17, waiting for transfers between devices, flip_fsdp(): lax.ppermute(value, 'fsdp', [(place, place ^ bits) for place in range(cou...  31.4 us
    pallas_call x4, Pallas kernels, mix_channels(): pl.pallas_call(body, out_shape=outs, grid_spec=pltpu.PrefetchScalarGridSp...  26.5 us
    pallas_call x3, Pallas kernels, share_partials(): pl.pallas_call(body, out_shape=[out, out], grid_spec=pltpu.PrefetchScalar...  25.3 us
    ppermute x17, starting transfers between devices, flip_fsdp(): lax.ppermute(value, 'fsdp', [(place, place ^ bits) for place in range(cou...  19 us
    ppermute x24, starting transfers between devices, next_chip(): return lax.ppermute(value, 'seq', route)  16.3 us
    pallas_call x1, Pallas kernels, scan_heads(): pl.pallas_call(body, out_shape=jax.ShapeDtypeStruct((tokens, width), jnp....  11.7 us
    all_to_all x1, waiting for transfers between devices, by_channel(): lax.all_to_all(slices, 'seq', split_axis=0, concat_axis=0, tiled=True)  7.96 us
  transfers between devices with their start and end apart: 50, of which 24 were waited for; matrix products, arithmetic and copies ran while one was open for 9% of the time, Pallas kernels for 21%

commit v1 on v0

--- a/solution.py
+++ b/solution.py
@@ -152,7 +152,9 @@
     return (tokens.astype(jnp.float32) + mixed).astype(jnp.bfloat16)
 
 
-VMEM_BYTES = 56 << 20
+VMEM_BYTES = 20 << 20
+SCAN_BYTES = 56 << 20
+FIRST_BYTES = 56 << 20
 
 
 def swap_cores(value):
@@ -171,16 +173,15 @@
     return lax.ppermute(value, "fsdp", [(place, place ^ bits) for place in range(count)])
 
 
-def share_partials(pieces, value_proj, gate_proj, small, where, chips, width):
+def share_partials(pieces, projections, plan, small, thin_places, where, chips, width, grant):
     depth, count = pieces[0].shape[1], pieces[0].shape[0]
     rows = count // (2 * chips)
     number = len(pieces)
-    tall = number * count
-    projections = [value for value in (value_proj, gate_proj) if value is not None]
-    thin_inputs = [] if small is None else [small]
-    thin_rows = 0 if small is None else number * (rows + rows // 2)
-    thin_width = 128 if small is None else small.shape[1]
-    total_rows = len(projections) * tall + thin_rows
+    thin_start = len(plan) * count
+    thins = len(thin_places)
+    thin_inputs = [small] if thins else []
+    maps_width = small.shape[1] - 128
+    total_rows = thin_start + thins * (rows + rows // 2)
 
     def body(where, *refs):
         row_refs, refs = refs[:number], refs[number:]
@@ -190,41 +191,39 @@
         chip = lax.rem(where[0] + chips - index, chips)
         first = core == 0
 
-        if small is not None:
+        if thins:
 
             @pl.when(index == 0)
             def _():
-                for place in range(number):
+                for place, piece in enumerate(thin_places):
                     thin[place * count : (place + 1) * count] = jnp.dot(
-                        row_refs[place][...], refs[0][...], preferred_element_type=jnp.float32
+                        row_refs[piece][...], refs[0][...], preferred_element_type=jnp.float32
                     ).astype(jnp.bfloat16)
 
             for out_ref, own in ((lent_ref, 1 - core), (kept_ref, core)):
-                for place in range(number):
+                for place in range(thins):
                     at = place * count + (own * chips + chip) * rows
-                    to = tall + place * rows
+                    to = thin_start + place * rows
                     out_ref[0, to : to + rows] = thin[
-                        pl.ds(pl.multiple_of(at, rows), rows), : thin_width - 128
+                        pl.ds(pl.multiple_of(at, rows), rows), :maps_width
                     ]
-                    to = tall + number * rows + place * rows // 2
+                    to = thin_start + thins * rows + place * rows // 2
                     halves = [
                         thin[
                             pl.ds(pl.multiple_of(at + part * rows // 2, rows // 2), rows // 2),
-                            thin_width - 128 :,
+                            maps_width:,
                         ]
                         for part in range(2)
                     ]
                     out_ref[0, to : to + rows // 2] = jnp.concatenate(halves, axis=1)
 
-        for which, weight_ref in enumerate(weight_refs):
-            base = which * (tall + thin_rows)
-            for place in range(number):
-                both = jnp.dot(
-                    row_refs[place][...], weight_ref[...], preferred_element_type=jnp.float32
-                ).astype(jnp.bfloat16)
-                at = slice(base + place * count, base + (place + 1) * count)
-                kept_ref[0, at] = jnp.where(first, both[:, :width], both[:, width:])
-                lent_ref[0, at] = jnp.where(first, both[:, width:], both[:, :width])
+        for place, (which, piece) in enumerate(plan):
+            both = jnp.dot(
+                row_refs[piece][...], weight_refs[which][...], preferred_element_type=jnp.float32
+            ).astype(jnp.bfloat16)
+            at = slice(place * count, (place + 1) * count)
+            kept_ref[0, at] = jnp.where(first, both[:, :width], both[:, width:])
+            lent_ref[0, at] = jnp.where(first, both[:, width:], both[:, :width])
 
     out = jax.ShapeDtypeStruct((chips, total_rows, width), jnp.bfloat16)
     return pl.pallas_call(
@@ -242,11 +241,9 @@
             ]
             + [pl.BlockSpec(value.shape, lambda i, where: (0, 0)) for value in thin_inputs],
             out_specs=[pl.BlockSpec((1, total_rows, width), lambda i, where: (i, 0, 0))] * 2,
-            scratch_shapes=[
-                pltpu.VMEM((16 if small is None else tall, thin_width), jnp.bfloat16)
-            ],
+            scratch_shapes=[pltpu.VMEM((max(1, thins) * count, maps_width + 128), jnp.bfloat16)],
         ),
-        compiler_params=pltpu.CompilerParams(vmem_limit_bytes=VMEM_BYTES),
+        compiler_params=pltpu.CompilerParams(vmem_limit_bytes=grant),
         name="share_partials",
     )(where, *pieces, *projections, *thin_inputs)
 
@@ -268,7 +265,7 @@
     return kept, got, passed[0]
 
 
-def scan_heads(order, trios, groups, thin, thin_swapped, ages, taps, state_taps, bias, rate, skip, sizes):
+def scan_heads(order, trios, groups, thin_groups, thin, thin_swapped, starts, taps, state_taps, bias, rate, skip, sizes):
     stretches, rows, quarters, width = sizes
     span = rows * quarters
     tokens = stretches * span
@@ -279,10 +276,17 @@
     flat = [value for trio in trios for value in trio]
     number = len(flat)
 
-    def body(order, *refs):
+    def body(order, starts_ref, *refs):
         trio_refs, refs = refs[:number], refs[number:]
-        thin_ref, swapped_ref, ages_ref, taps_ref, state_taps_ref, bias_ref = refs[:6]
-        rate_ref, skip_ref, out_ref, values, maps, steps, state = refs[6:]
+        thin_ref, swapped_ref, taps_ref, state_taps_ref, bias_ref = refs[:5]
+        rate_ref, skip_ref, out_ref, values, maps, steps, state, ages = refs[5:]
+        token = lax.broadcasted_iota(jnp.int32, (stretches, span), 0) * span
+        token = token + lax.broadcasted_iota(jnp.int32, (stretches, span), 1)
+        age_rows = jnp.full((stretches, span), tokens, jnp.int32)
+        for document in range(starts.shape[0]):
+            since = token - starts_ref[document]
+            age_rows = jnp.where(since >= 0, jnp.minimum(age_rows, since), age_rows)
+        ages[...] = age_rows.astype(jnp.float32)
         first_head, chip, core = (order[quarters + place] for place in range(3))
         values[:8] = jnp.zeros((8, width), jnp.float32)
         maps[:8] = jnp.zeros((8, 2 * N), jnp.float32)
@@ -308,7 +312,7 @@
             for away in range(chips):
                 stretch = own_core * chips + lax.rem(chip + chips - away, chips)
                 base = 0
-                for members in groups:
+                for members in thin_groups:
                     for place, k in enumerate(members):
                         to = pl.multiple_of(stretch * span + order[k] * rows, rows)
                         at = base + place * rows
@@ -345,7 +349,8 @@
 
         def chunk(index, carry):
             start = pl.multiple_of(index * span, span)
-            age = ages_ref[pl.ds(start, span), :]
+            age = jnp.broadcast_to(ages[pl.ds(index, 1), :], (span, span)).T.astype(jnp.int32)
+            age = age[:, :1]
             last_age = age[span - 1 :]
             inputs = convolve(values, taps_ref[...], start, age)
             both = convolve(maps, state_taps_ref[...], start, age)
@@ -396,32 +401,33 @@
 
         lax.fori_loop(0, stretches, chunk, 0)
 
-    whole = lambda value: pl.BlockSpec(value.shape, lambda i, order: (0,) * value.ndim)
+    whole = lambda value: pl.BlockSpec(value.shape, lambda i, order, starts: (0,) * value.ndim)
     trio_specs = [
-        pl.BlockSpec((1,) + value.shape[1:], lambda i, order: (0, 0, 0))
+        pl.BlockSpec((1,) + value.shape[1:], lambda i, order, starts: (0, 0, 0))
         if value.ndim == 3
         else whole(value)
         for value in flat
     ]
-    rest = (thin, thin_swapped, ages, taps, state_taps, bias, rate, skip)
+    rest = (thin, thin_swapped, taps, state_taps, bias, rate, skip)
     return pl.pallas_call(
         body,
         out_shape=jax.ShapeDtypeStruct((tokens, width), jnp.float32),
         grid_spec=pltpu.PrefetchScalarGridSpec(
-            num_scalar_prefetch=1,
+            num_scalar_prefetch=2,
             grid=(1,),
             in_specs=trio_specs + [whole(value) for value in rest],
-            out_specs=pl.BlockSpec((tokens, width), lambda i, order: (0, 0)),
+            out_specs=pl.BlockSpec((tokens, width), lambda i, order, starts: (0, 0)),
             scratch_shapes=[
                 pltpu.VMEM((tokens + 8, width), jnp.float32),
                 pltpu.VMEM((tokens + 8, 2 * N), jnp.float32),
                 pltpu.VMEM((tokens, 128), jnp.float32),
                 pltpu.VMEM((N, width), jnp.float32),
+                pltpu.VMEM((stretches, span), jnp.float32),
             ],
         ),
-        compiler_params=pltpu.CompilerParams(vmem_limit_bytes=VMEM_BYTES),
+        compiler_params=pltpu.CompilerParams(vmem_limit_bytes=SCAN_BYTES),
         name="scan_heads",
-    )(order, *flat, *rest)
+    )(order, starts, *flat, *rest)
 
 
 def gate_outputs(order, outputs, trios, groups, offsets, sizes):
@@ -472,15 +478,16 @@
             + [whole((stretches, quarters, rows, width))],
             out_specs=[whole(shape)] * 4,
         ),
-        compiler_params=pltpu.CompilerParams(vmem_limit_bytes=VMEM_BYTES),
+        compiler_params=pltpu.CompilerParams(vmem_limit_bytes=SCAN_BYTES),
         name="gate_outputs",
     )(order, *flat, outputs.reshape(stretches, quarters, rows, width))
 
 
-def mix_channels(order, near, far, away, so_far, gains, own_proj, other_proj, sizes):
+def mix_channels(order, pairs, away, so_far, gains, own_proj, other_proj, sizes):
     stretches, rows, quarters, width = sizes
     half, chips = rows // 2, stretches // 2
-    count = near.shape[1]
+    count = pairs[0].shape[1]
+    number = len(pairs) // 2
     channels, columns = own_proj.shape
     last = so_far is not None
     so_far = list(so_far) if last else []
@@ -489,27 +496,33 @@
         chip, core = order[quarters + 1], order[quarters + 2]
         return 2 * lax.rem(chip + chips - away - i // 2, chips) + lax.rem(core + i, 2)
 
-    def body(order, near_ref, far_ref, gains_ref, own_ref, other_ref, *refs):
+    def body(order, *refs):
+        pair_refs, refs = refs[: len(pairs)], refs[len(pairs) :]
+        gains_ref, own_ref, other_ref, refs = *refs[:3], refs[3:]
         before, refs = refs[: len(so_far)], refs[len(so_far) :]
-        total, squares = refs[-2:] if last else refs
+        totals = refs[5:] if last else refs
         index = pl.program_id(0)
 
         @pl.when(index == 0)
         def _():
-            total[...] = before[0][...] if last else jnp.zeros_like(total)
-            squares[...] = before[1][...] if last else jnp.zeros_like(squares)
-
-        block = jnp.where(index < 2, near_ref[0], far_ref[0]).astype(jnp.float32)
-        squares[...] += jnp.broadcast_to(
-            jnp.sum(block * block, axis=1, keepdims=True), squares.shape
-        )
-        gained = (block * gains_ref[pl.ds(owner_of(index, order), 1), :]).astype(jnp.bfloat16)
-        for side, weights_ref in enumerate((own_ref, other_ref)):
-            total[:, side * columns : (side + 1) * columns] += jnp.dot(
-                gained, weights_ref[...], preferred_element_type=jnp.float32
+            for place, total in enumerate(totals):
+                total[...] = before[place][...] if last else jnp.zeros_like(total)
+
+        for part in range(number):
+            near_ref, far_ref = pair_refs[2 * part : 2 * part + 2]
+            total, squares = totals[2 * part : 2 * part + 2]
+            block = jnp.where(index < 2, near_ref[0], far_ref[0]).astype(jnp.float32)
+            squares[...] += jnp.broadcast_to(
+                jnp.sum(block * block, axis=1, keepdims=True), squares.shape
             )
+            gain = gains_ref[pl.ds(owner_of(index, order), 1), :]
+            gained = (block * gain).astype(jnp.bfloat16)
+            for side, weights_ref in enumerate((own_ref, other_ref)):
+                total[:, side * columns : (side + 1) * columns] += jnp.dot(
+                    gained, weights_ref[...], preferred_element_type=jnp.float32
+                )
         if last:
-            rounded = refs[4]
+            total, squares, rounded = *totals, refs[4]
 
             @pl.when(index == pl.num_programs(0) - 1)
             def _():
@@ -517,17 +530,18 @@
                 rounded[...] = (total[...] * factor).astype(jnp.bfloat16)
                 left_kept, left_sent, right_kept, right_sent = refs[:4]
                 for k in range(4):
-                    for chip in range(chips):
-                        at = pl.multiple_of((chip * quarters + order[k]) * half, half)
+                    for away in range(chips):
+                        goal = lax.rem(order[quarters + 1] + away, chips)
+                        at = pl.multiple_of((goal * quarters + order[k]) * half, half)
                         value = rounded[pl.ds(at, half), :]
-                        (left_sent if k % 2 else left_kept)[k // 2, chip] = value[:, :columns]
-                        (right_sent if k // 2 else right_kept)[k % 2, chip] = value[:, columns:]
+                        (left_sent if k % 2 else left_kept)[k // 2, away] = value[:, :columns]
+                        (right_sent if k // 2 else right_kept)[k % 2, away] = value[:, columns:]
 
     whole = lambda shape: pl.BlockSpec(shape, lambda i, order: (0,) * len(shape))
     sums = [
         jax.ShapeDtypeStruct((count, 2 * columns), jnp.float32),
         jax.ShapeDtypeStruct((count, 128), jnp.float32),
-    ]
+    ] * number
     part = jax.ShapeDtypeStruct((2, chips, half, columns), jnp.bfloat16)
     outs = [part] * 4 if last else sums
     scratch = [
@@ -535,26 +549,25 @@
         *(pltpu.VMEM(value.shape, value.dtype) for value in sums),
     ]
     weights_spec = pl.BlockSpec((width, columns), lambda i, order: (owner_of(i, order), 0))
+    pair_specs = [
+        pl.BlockSpec((1, count, width), lambda i, order: (jnp.minimum(i, 1), 0, 0)),
+        pl.BlockSpec((1, count, width), lambda i, order: (jnp.maximum(i - 2, 0), 0, 0)),
+    ]
     return pl.pallas_call(
         body,
         out_shape=outs,
         grid_spec=pltpu.PrefetchScalarGridSpec(
             num_scalar_prefetch=1,
             grid=(4,),
-            in_specs=[
-                pl.BlockSpec((1, count, width), lambda i, order: (jnp.minimum(i, 1), 0, 0)),
-                pl.BlockSpec((1, count, width), lambda i, order: (jnp.maximum(i - 2, 0), 0, 0)),
-                whole(gains.shape),
-                weights_spec,
-                weights_spec,
-            ]
+            in_specs=pair_specs * number
+            + [whole(gains.shape), weights_spec, weights_spec]
             + [whole(value.shape) for value in so_far],
             out_specs=[whole(value.shape) for value in outs],
             scratch_shapes=scratch if last else [],
         ),
         compiler_params=pltpu.CompilerParams(vmem_limit_bytes=VMEM_BYTES),
         name="mix_channels",
-    )(order, near, far, gains, own_proj, other_proj, *so_far)
+    )(order, *pairs, gains, own_proj, other_proj, *so_far)
 
 
 def add_tokens(order, tokens, pieces, sizes):
@@ -569,15 +582,14 @@
 
             @pl.when(core == at_core)
             def _():
-                for place in range(len(pieces)):
-                    part, k = place // quarters, place % quarters
+                for part, k in ((part, k) for part in range(2) for k in range(quarters)):
                     at = pl.ds(pl.multiple_of(order[k] * rows + part * half, half), half)
                     for side in range(2):
                         start = (at_core if side == 0 else 1 - at_core) * columns
                         across = slice(start, start + columns)
                         out_ref[at, across] = (
                             tokens_ref[at, across].astype(jnp.float32)
-                            + refs[place][side].astype(jnp.float32)
+                            + refs[k][2 * part + side].astype(jnp.float32)
                         ).astype(jnp.bfloat16)
 
     whole = lambda value: pl.BlockSpec(value.shape, lambda i, order: (0,) * value.ndim)
@@ -593,9 +605,6 @@
         compiler_params=pltpu.CompilerParams(vmem_limit_bytes=VMEM_BYTES),
         name="add_tokens",
     )(order, tokens, *pieces)
-
-
-VALUE_GROUPS = ((0,), (1, 2, 3))
 
 
 def by_channel(
@@ -638,13 +647,7 @@
     small = jnp.concatenate(
         [state_cols, step_proj, jnp.zeros((depth, 128 - head_count), jnp.bfloat16)], axis=1
     )
-    starts = jnp.cumsum(doc_lengths) - doc_lengths
-    index = jnp.arange(total_tokens, dtype=jnp.int32)[:, None]
-    ages = jnp.min(
-        jnp.where(starts[None, :] <= index, index - starts[None, :], total_tokens),
-        axis=1,
-        keepdims=True,
-    )
+    starts = (jnp.cumsum(doc_lengths) - doc_lengths).astype(jnp.int32)
     own_part = lambda value: lax.dynamic_slice_in_dim(value, seq_index * heads, heads, 0)
     lanes = lambda value: jnp.pad(own_part(value), (0, 128 - heads))[None, :]
     bias, rate = lanes(step_bias), lanes(decay_rate)
@@ -671,59 +674,62 @@
     own = lax.all_to_all(slices, "seq", split_axis=0, concat_axis=0, tiled=True).reshape(
         stretches * rows, depth
     )
-    own, small, ages, bias, rate, skip, taps, state_taps, order, where = lax.optimization_barrier(
-        (own, small, ages, bias, rate, skip, taps, state_taps, order, where)
+    own, small, starts, bias, rate, skip, taps, state_taps, order, where = lax.optimization_barrier(
+        (own, small, starts, bias, rate, skip, taps, state_taps, order, where)
     )
 
     near = [flip_fsdp(own, 1), flip_fsdp(own, 2)]
     near[0], near[1], again = lax.optimization_barrier((near[0], near[1], own))
     pieces = [own, *near, flip_fsdp(again, 3)]
 
-    def reduced(inputs, *weights):
-        lent, kept = share_partials(inputs, *weights, where, chips, width)
+    def reduced(members, projections, plan, thin_places=(), grant=VMEM_BYTES):
+        lent, kept = share_partials(
+            [pieces[k] for k in members], projections, plan, small, thin_places, where,
+            chips, width, grant,
+        )
         return ring_reduce(kept, lent)
 
-    ahead, behind = VALUE_GROUPS
-    later = [pieces[k] for k in behind]
-    first = reduced([pieces[k] for k in ahead], value_proj, gate_proj, small)
-    second = reduced(later, value_proj, None, small)
-    third = reduced(later, gate_proj, None, None)
-    thin = []
-    for members, trio in zip(VALUE_GROUPS, (first, second)):
-        begin = len(members) * stretches * rows
-        end = begin + len(members) * (rows + rows // 2)
-        thin.append(
-            add_up(trio[0][0, begin:end], trio[1][0, begin:end], trio[2][begin:end]).astype(
+    count = stretches * rows
+    first = reduced((0,), [value_proj, gate_proj], ((0, 0), (1, 0)), (0,), FIRST_BYTES)
+    second = reduced((3, 1, 2), [value_proj], ((0, 0),), (0, 1, 2))
+    third = reduced((1, 2), [value_proj], ((0, 0), (0, 1)))
+    fourth = reduced((1, 2, 3), [gate_proj], ((0, 0), (0, 1), (0, 2)))
+    value_groups, thin_groups = ((0,), (3,), (1, 2)), ((0,), (3, 1, 2))
+    gate_groups, gate_starts = ((0,), (1, 2, 3)), (count, 0)
+    thin = jnp.concatenate(
+        [
+            add_up(trio[0][0, start:], trio[1][0, start:], trio[2][start:]).astype(
                 jnp.bfloat16
             )
-        )
-    thin = jnp.concatenate(thin, axis=0)
+            for trio, start in ((first, 2 * count), (second, count))
+        ]
+    )
     spread = [thin]
-    for away in range(1, chips):
-        spread.append(next_chip(thin, away))
+    for _ in range(1, chips):
+        spread.append(next_chip(spread[-1]))
     thin = jnp.stack(spread)
     thin_swapped = swap_cores(thin)
     outputs = scan_heads(
-        order, (first, second), VALUE_GROUPS, thin, thin_swapped, ages, taps, state_taps,
+        order, (first, second, third), value_groups, thin_groups, thin, thin_swapped, starts, taps, state_taps,
         bias, rate, skip, sizes,
     )
-    gate_start = len(ahead) * (stretches * rows + rows + rows // 2)
-    parts = gate_outputs(
-        order, outputs, (first, third), VALUE_GROUPS, (gate_start, 0), sizes
-    )
+    parts = gate_outputs(order, outputs, (first, fourth), gate_groups, gate_starts, sizes)
     gains = mix_gain.reshape(stretches, width)
-    ended = []
+    sums, shares = [], []
     for part in range(2):
         flat = lambda value: value.reshape(total_tokens // 4, width)
         came = swap_cores(parts[2 + part])
         blocks = [jnp.stack([flat(parts[part]), flat(came)])]
         for _ in range(1, chips):
             blocks.append(next_chip(blocks[-1]))
-        so_far = mix_channels(
-            order, *blocks[:2], 0, None, gains, out_proj, other_proj, sizes
-        )
+        shares.append(blocks)
+    so_far = mix_channels(
+        order, shares[0][:2] + shares[1][:2], 0, None, gains, out_proj, other_proj, sizes
+    )
+    for part in range(2):
         left_kept, left_sent, right_kept, right_sent = mix_channels(
-            order, *blocks[2:], 2, so_far, gains, out_proj, other_proj, sizes
+            order, shares[part][2:], 2, so_far[2 * part : 2 * part + 2], gains, out_proj,
+            other_proj, sizes,
         )
         left_got = flip_fsdp(left_sent, 1)
         right_got = flip_fsdp(right_sent, 2)
@@ -731,24 +737,26 @@
         right_sum = add_up(right_kept[1], right_got[1]).astype(jnp.bfloat16)
         left_more = flip_fsdp(left_sum, 2)
         right_more = flip_fsdp(right_sum, 1)
-        summed = jnp.stack(
-            [
-                add_up(left_kept[0], left_got[0], left_more).astype(jnp.bfloat16),
-                add_up(right_kept[0], right_got[0], right_more).astype(jnp.bfloat16),
-            ],
-            axis=1,
-        )
-        to_chip = lambda away: lax.dynamic_index_in_dim(summed, (chip + away) % chips, 0, False)
-        arrived = [to_chip(0)]
+        sums.append((left_kept[0], left_got[0], left_more, right_kept[0], right_got[0], right_more))
+
+    def to_chip(away):
+        pick = lambda terms: add_up(*(term[away] for term in terms)).astype(jnp.bfloat16)
+        return jnp.stack([pick(terms[side : side + 3]) for terms in sums for side in (0, 3)])
+
+    arrived = [to_chip(0)]
+    for away in range(1, chips):
+        arrived.append(next_chip(to_chip(away), away))
+
+    def from_chip(other):
+        back = (chip + chips - other) % chips
+        value = arrived[0]
         for away in range(1, chips):
-            arrived.append(next_chip(to_chip(away), away))
-        arrived = jnp.stack(arrived)
-        from_chip = lambda other: lax.dynamic_index_in_dim(
-            arrived, (chip + chips - other) % chips, 0, False
-        )
-        ended.append(from_chip(fsdp_index))
-        for k in range(1, quarters):
-            ended.append(flip_fsdp(from_chip(fsdp_index ^ k), k))
+            value = jnp.where(back == away, arrived[away], value)
+        return value
+
+    ended = [from_chip(fsdp_index)]
+    for k in range(1, quarters):
+        ended.append(flip_fsdp(from_chip(fsdp_index ^ k), k))
     return add_tokens(order, tokens, ended, sizes)
 
 

time: 284 us -> 275 us (0.968)
  waiting for transfers between devices: 137 us -> 169 us
  Pallas kernels: 70.1 us -> 54.5 us
  starting transfers between devices: 47 us -> 32.1 us
  other arithmetic: 13.7 us -> 7.25 us
  local copies, waits for them, and re-layouts: 14.2 us -> 10.2 us
    ppermute x24, waiting for transfers between devices: 90.7 us -> 114 us  [next_chip(): return lax.ppermute(value, 'seq', route)]
    pallas_call x4 -> x3, Pallas kernels: 26.5 us -> 15.6 us  [mix_channels(): pl.pallas_call(body, out_shape=outs, grid_spec=pltpu.PrefetchScalarGridSp...]
    ppermute x24, starting transfers between devices: 16.3 us -> 5.5 us  [next_chip(): return lax.ppermute(value, 'seq', route)]
    ppermute x17 -> x14, waiting for transfers between devices: 31.4 us -> 38.8 us  [flip_fsdp(): lax.ppermute(value, 'fsdp', [(place, place ^ bits) for place in range(cou...]
    pallas_call x3 -> x4, Pallas kernels: 25.3 us -> 21.2 us  [share_partials(): pl.pallas_call(body, out_shape=[out, out], grid_spec=pltpu.PrefetchScalar...]
    convert_element_type x9 -> x12, other arithmetic: 5.23 us -> 1.15 us  [ring_reduce(): sent = add_up(kept[step], got[step], *passed).astype(jnp.bfloat16)]
    ppermute x17 -> x14, starting transfers between devices: 19 us -> 15.4 us  [flip_fsdp(): lax.ppermute(value, 'fsdp', [(place, place ^ bits) for place in range(cou...]
    all_to_all x1, waiting for transfers between devices: 4.34 us -> 7.24 us  [by_channel(): lax.all_to_all(tokens.reshape(quarters, rows, features), 'fsdp', split_ax...]
  transfers between devices with their start and end apart: 50 -> 48, of which waited for: 24 -> 31; matrix products, arithmetic and copies ran while one was open for 9% -> 5% of each run, Pallas kernels for 21% -> 16%
where the time goes in v1:
time: 275 us; the launch traced here: 274 us
  waiting for transfers between devices  169 us (61%)
  Pallas kernels  54.5 us (20%)
  starting transfers between devices  32.1 us (12%)
  local copies, waits for them, and re-layouts  10.2 us (4%)
  other arithmetic  7.25 us (3%)
    ppermute x24, waiting for transfers between devices, next_chip(): return lax.ppermute(value, 'seq', route)  114 us
    ppermute x14, waiting for transfers between devices, flip_fsdp(): lax.ppermute(value, 'fsdp', [(place, place ^ bits) for place in range(cou...  38.8 us
    pallas_call x4, Pallas kernels, share_partials(): pl.pallas_call(body, out_shape=[out, out], grid_spec=pltpu.PrefetchScalar...  21.2 us
    pallas_call x3, Pallas kernels, mix_channels(): pl.pallas_call(body, out_shape=outs, grid_spec=pltpu.PrefetchScalarGridSp...  15.6 us
    ppermute x14, starting transfers between devices, flip_fsdp(): lax.ppermute(value, 'fsdp', [(place, place ^ bits) for place in range(cou...  15.4 us
    pallas_call x1, Pallas kernels, scan_heads(): pl.pallas_call(body, out_shape=jax.ShapeDtypeStruct((tokens, width), jnp....  12.4 us
    all_to_all x1, waiting for transfers between devices, by_channel(): lax.all_to_all(tokens.reshape(quarters, rows, features), 'fsdp', split_ax...  7.24 us
    all_to_all x1, waiting for transfers between devices, by_channel(): lax.all_to_all(slices, 'seq', split_axis=0, concat_axis=0, tiled=True)  6.65 us
  transfers between devices with their start and end apart: 48, of which 31 were waited for; matrix products, arithmetic and copies ran while one was open for 5% of the time, Pallas kernels for 16%

profile of v1, /device:TPU:0, one launch (start us, length us, event | category | flops | bytes accessed | tf_op | source)
XLA Modules:
  0.0 274.2 jit_solution(14625086883347264010)
XLA Ops:
  0.0 5.3 %all-to-all-start = ((bf16[4,32,2048]{2,1,0:T(8,128)(2,1)}), bf16[4,32,2048]{2,1,0:T(8,128)(2,1)S(1)}, u32[]{:S(2)}, u32[]{:S(2)}) async-start(bf16[4,32,2048]{2,1,0:T(8,128)(2,1)} %bitcast.151), calls=%async_computation | async-start | bytes 1048576 | tf_op jit(solution)/shard_map/all_to_all | solution.py:659
  6.1 7.2 %all-to-all-done = bf16[4,32,2048]{2,1,0:T(8,128)(2,1)S(1)} async-done(((bf16[4,32,2048]{2,1,0:T(8,128)(2,1)}), bf16[4,32,2048]{2,1,0:T(8,128)(2,1)S(1)}, u32[]{:S(2)}, u32[]{:S(2)}) %all-to-all-start) | async-done | bytes 524320 | tf_op jit(solution)/shard_map/all_to_all | solution.py:659
  14.7 4.9 %all-to-all-start.1 = ((bf16[8,32,1024]{2,1,0:T(8,128)(2,1)}), bf16[8,32,1024]{2,1,0:T(8,128)(2,1)S(1)}, u32[]{:S(2)}, u32[]{:S(2)}) async-start(bf16[8,32,1024]{2,1,0:T(8,128)(2,1)} %bitcast.1), calls=%async_computation.1 | async-start | bytes 1048576 | tf_op jit(solution)/shard_map/all_to_all | solution.py:674
  28.3 6.6 %all-to-all-done.1 = bf16[8,32,1024]{2,1,0:T(8,128)(2,1)S(1)} async-done(((bf16[8,32,1024]{2,1,0:T(8,128)(2,1)}), bf16[8,32,1024]{2,1,0:T(8,128)(2,1)S(1)}, u32[]{:S(2)}, u32[]{:S(2)}) %all-to-all-start.1) | async-done | bytes 524320 | tf_op jit(solution)/shard_map/all_to_all | solution.py:674
  35.7 8.6 %share_partials.4 = (bf16[4,560,256]{2,1,0:T(8,128)(2,1)}, bf16[4,560,256]{2,1,0:T(8,128)(2,1)}) custom-call(s32[2]{0:T(128)} %pad_add_fusion.where, bf16[256,1024]{1,0:T(8,128)(2,1)} %bitcast.153, bf16[1024,2048]{1,0:T(8,128)(2,1)} %refs_2_.3, bf16[1024,2048]{1,0:T(8,128)(2,1)} %refs_3_.4, bf16[1024,384]{1,0:T(8,128)(2,1)} %maximum_maximum_fusion.refs_3_.refs_4_), custom_call_target="tpu_custom_call" | custom-call | tf_op jit(solution)/shard_map/share_partials/pallas_call | solution.py:229
  46.4 12.5 %collective-permute-done.4.refs_0_.refs_1_ = bf16[256,1024]{1,0:T(8,128)(2,1)S(1)} collective-permute-done((bf16[256,1024]{1,0:T(8,128)(2,1)}, bf16[256,1024]{1,0:T(8,128)(2,1)S(1)}, u32[]{:S(2)}, u32[]{:S(2)}) %collective-permute-start.4) | collective-permute-done | bytes 524320 | tf_op jit(solution)/shard_map/ppermute | solution.py:173
  61.5 12.7 %collective-permute-done.6.refs_2_.refs_0_ = bf16[256,1024]{1,0:T(8,128)(2,1)S(1)} collective-permute-done((bf16[256,1024]{1,0:T(8,128)(2,1)}, bf16[256,1024]{1,0:T(8,128)(2,1)S(1)}, u32[]{:S(2)}, u32[]{:S(2)}) %collective-permute-start.6) | collective-permute-done | bytes 524320 | tf_op jit(solution)/shard_map/ppermute | solution.py:173
  74.2 3.8 %share_partials.6 = (bf16[4,400,256]{2,1,0:T(8,128)(2,1)S(1)}, bf16[4,400,256]{2,1,0:T(8,128)(2,1)S(1)}) custom-call(s32[2]{0:T(128)S(1)} %copy-done.9, bf16[256,1024]{1,0:T(8,128)(2,1)S(1)} %collective-permute-done.6.refs_2_.refs_0_, bf16[256,1024]{1,0:T(8,128)(2,1)S(1)} %collective-permute-done.4.refs_0_.refs_1_, ...), custom_call_target="tpu_custom_call" | custom-call | tf_op jit(solution)/shard_map/share_partials/pallas_call | solution.py:229
  78.4 5.0 %share_partials.5 = (bf16[4,768,256]{2,1,0:T(8,128)(2,1)S(1)}, bf16[4,768,256]{2,1,0:T(8,128)(2,1)S(1)}) custom-call(s32[2]{0:T(128)S(1)} %copy-done.9, bf16[256,1024]{1,0:T(8,128)(2,1)S(1)} %collective-permute-done.4.refs_0_.refs_1_, bf16[256,1024]{1,0:T(8,128)(2,1)S(1)} %collective-permute-done.5.refs_1_.refs_2_, ...), custom_call_target="tpu_custom_call" | custom-call | tf_op jit(solution)/shard_map/share_partials/pallas_call | solution.py:229
  83.9 5.5 %collective-permute-done.1 = bf16[560,256]{1,0:T(8,128)(2,1)S(1)} collective-permute-done((bf16[560,256]{1,0:T(8,128)(2,1)S(1)}, bf16[560,256]{1,0:T(8,128)(2,1)S(1)}, u32[]{:S(2)}, u32[]{:S(2)}) %collective-permute-start.1) | collective-permute-done | bytes 286752 | tf_op jit(solution)/shard_map/ppermute | solution.py:168
  89.7 11.3 %collective-permute-done.2 = bf16[560,256]{1,0:T(8,128)(2,1)S(1)} collective-permute-done((bf16[560,256]{1,0:T(8,128)(2,1)S(1)}, bf16[560,256]{1,0:T(8,128)(2,1)S(1)}, u32[]{:S(2)}, u32[]{:S(2)}) %collective-permute-start.2) | collective-permute-done | bytes 286752 | tf_op jit(solution)/shard_map/ppermute | solution.py:168
  101.2 3.8 %share_partials.7 = (bf16[4,512,256]{2,1,0:T(8,128)(2,1)S(1)}, bf16[4,512,256]{2,1,0:T(8,128)(2,1)S(1)}) custom-call(s32[2]{0:T(128)S(1)} %copy-done.9, bf16[256,1024]{1,0:T(8,128)(2,1)S(1)} %collective-permute-done.4.refs_0_.refs_1_, bf16[256,1024]{1,0:T(8,128)(2,1)S(1)} %collective-permute-done.5.refs_1_.refs_2_, bf16[1024,2048]{1,0:T(8,128)(2,1)S(1)} %copy-done.1), custom_call_target="tpu_custom_call" | custom-call | tf_op jit(solution)/shard_map/share_partials/pallas_call | solution.py:229
  105.3 4.9 %collective-permute-done.3.refs_2_ = bf16[560,256]{1,0:T(8,128)(2,1)S(1)} collective-permute-done((bf16[560,256]{1,0:T(8,128)(2,1)S(1)}, bf16[560,256]{1,0:T(8,128)(2,1)S(1)}, u32[]{:S(2)}, u32[]{:S(2)}) %collective-permute-start.3) | collective-permute-done | bytes 286752 | tf_op jit(solution)/shard_map/ppermute | solution.py:168
  110.2 4.6 %collective-permute-done.13 = bf16[400,256]{1,0:T(8,128)(2,1)S(1)} collective-permute-done((bf16[400,256]{1,0:T(8,128)(2,1)S(1)}, bf16[400,256]{1,0:T(8,128)(2,1)S(1)}, u32[]{:S(2)}, u32[]{:S(2)}) %collective-permute-start.13) | collective-permute-done | bytes 204832 | tf_op jit(solution)/shard_map/ppermute | solution.py:168
  115.5 9.2 %collective-permute-done.14.refs_5_ = bf16[400,256]{1,0:T(8,128)(2,1)S(1)} collective-permute-done((bf16[400,256]{1,0:T(8,128)(2,1)S(1)}, bf16[400,256]{1,0:T(8,128)(2,1)S(1)}, u32[]{:S(2)}, u32[]{:S(2)}) %collective-permute-start.14) | collective-permute-done | bytes 204832 | tf_op jit(solution)/shard_map/ppermute | solution.py:168
  125.0 10.2 %collective-permute-done.19 = bf16[192,256]{1,0:T(8,128)(2,1)S(1)} collective-permute-done((bf16[192,256]{1,0:T(8,128)(2,1)S(1)}, bf16[192,256]{1,0:T(8,128)(2,1)S(1)}, u32[]{:S(2)}, u32[]{:S(2)}) %collective-permute-start.19) | collective-permute-done | bytes 98336 | tf_op jit(solution)/shard_map/ppermute | solution.py:168
  135.4 7.5 %collective-permute-done.20 = bf16[192,256]{1,0:T(8,128)(2,1)S(1)} collective-permute-done((bf16[192,256]{1,0:T(8,128)(2,1)S(1)}, bf16[192,256]{1,0:T(8,128)(2,1)S(1)}, u32[]{:S(2)}, u32[]{:S(2)}) %collective-permute-start.20) | collective-permute-done | bytes 98336 | tf_op jit(solution)/shard_map/ppermute | solution.py:168
  143.1 10.3 %collective-permute-done.21 = bf16[192,256]{1,0:T(8,128)(2,1)S(1)} collective-permute-done((bf16[192,256]{1,0:T(8,128)(2,1)S(1)}, bf16[192,256]{1,0:T(8,128)(2,1)S(1)}, u32[]{:S(2)}, u32[]{:S(2)}) %collective-permute-start.21) | collective-permute-done | bytes 98336 | tf_op jit(solution)/shard_map/ppermute | solution.py:168
  153.9 4.2 %collective-permute-done.17 = bf16[512,256]{1,0:T(8,128)(2,1)S(1)} collective-permute-done((bf16[512,256]{1,0:T(8,128)(2,1)S(1)}, bf16[512,256]{1,0:T(8,128)(2,1)S(1)}, u32[]{:S(2)}, u32[]{:S(2)}) %collective-permute-start.17) | collective-permute-done | bytes 262176 | tf_op jit(solution)/shard_map/ppermute | solution.py:168
  158.2 14.6 %collective-permute-done.18.refs_8_ = bf16[512,256]{1,0:T(8,128)(2,1)S(1)} collective-permute-done((bf16[512,256]{1,0:T(8,128)(2,1)S(1)}, bf16[512,256]{1,0:T(8,128)(2,1)S(1)}, u32[]{:S(2)}, u32[]{:S(2)}) %collective-permute-start.18) | collective-permute-done | bytes 262176 | tf_op jit(solution)/shard_map/ppermute | solution.py:168
  174.2 12.4 %scan_heads.1 = f32[1024,256]{1,0:T(8,128)} custom-call(s32[7]{0:T(128)} %stack.85.order, s32[16]{0:T(128)} %sub.19.starts_ref, bf16[4,560,256]{2,1,0:T(8,128)(2,1)} %get-tuple-element.46.refs_0_, bf16[4,560,256]{2,1,0:T(8,128)(2,1)} %copy-done.11, bf16[560,256]{1,0:T(8,128)(2,1)} %copy-done.17, bf16[4,400,256]{2,1,0:T(8,128)(2,1)} %copy-done.6, ...), custom_call_target="tpu_custom_call" | custom-call | tf_op jit(solution)/shard_map/scan_heads/pallas_call | solution.py:412
  187.4 3.8 %gate_outputs.1 = (bf16[4,4,16,256]{3,2,1,0:T(8,128)(2,1)}, bf16[4,4,16,256]{3,2,1,0:T(8,128)(2,1)}, bf16[4,4,16,256]{3,2,1,0:T(8,128)(2,1)}, bf16[4,4,16,256]{3,2,1,0:T(8,128)(2,1)}) custom-call(s32[7]{0:T(128)} %stack.85.order, bf16[4,560,256]{2,1,0:T(8,128)(2,1)} %get-tuple-element.46.refs_0_, bf16[4,560,256]{2,1,0:T(8,128)(2,1)} %copy-done.11, ...), custom_call_target="tpu_custom_call" | custom-call | tf_op jit(solution)/shard_map/gate_outputs/pallas_call | solution.py:468
  196.4 8.3 %collective-permute-done.24.refs_1_ = bf16[2,256,256]{2,1,0:T(8,128)(2,1)S(1)} collective-permute-done((bf16[2,256,256]{2,1,0:T(8,128)(2,1)S(1)}, bf16[2,256,256]{2,1,0:T(8,128)(2,1)S(1)}, u32[]{:S(2)}, u32[]{:S(2)}) %collective-permute-start.24) | collective-permute-done | bytes 262176 | tf_op jit(solution)/shard_map/ppermute | solution.py:168
  204.7 5.7 %collective-permute-done.29.refs_3_ = bf16[2,256,256]{2,1,0:T(8,128)(2,1)} collective-permute-done((bf16[2,256,256]{2,1,0:T(8,128)(2,1)S(1)}, bf16[2,256,256]{2,1,0:T(8,128)(2,1)}, u32[]{:S(2)}, u32[]{:S(2)}) %collective-permute-start.29) | collective-permute-done | bytes 262176 | tf_op jit(solution)/shard_map/ppermute | solution.py:168
  210.5 5.5 %collective-permute-done.25.refs_0_ = bf16[2,256,256]{2,1,0:T(8,128)(2,1)S(1)} collective-permute-done((bf16[2,256,256]{2,1,0:T(8,128)(2,1)S(1)}, bf16[2,256,256]{2,1,0:T(8,128)(2,1)S(1)}, u32[]{:S(2)}, u32[]{:S(2)}) %collective-permute-start.25) | collective-permute-done | bytes 262176 | tf_op jit(solution)/shard_map/ppermute | solution.py:168
  216.0 5.7 %collective-permute-done.34.refs_0_ = bf16[2,256,256]{2,1,0:T(8,128)(2,1)S(1)} collective-permute-done((bf16[2,256,256]{2,1,0:T(8,128)(2,1)}, bf16[2,256,256]{2,1,0:T(8,128)(2,1)S(1)}, u32[]{:S(2)}, u32[]{:S(2)}) %collective-permute-start.34) | collective-permute-done | bytes 262176 | tf_op jit(solution)/shard_map/ppermute | solution.py:168
  221.7 5.7 %mix_channels.3 = (f32[256,2048]{1,0:T(8,128)S(1)}, f32[256,128]{1,0:T(8,128)S(1)}, f32[256,2048]{1,0:T(8,128)S(1)}, f32[256,128]{1,0:T(8,128)S(1)}) custom-call(s32[7]{0:T(128)S(1)} %copy-done.8, bf16[2,256,256]{2,1,0:T(8,128)(2,1)S(1)} %pad_maximum_fusion.2.refs_0_, bf16[2,256,256]{2,1,0:T(8,128)(2,1)S(1)} %collective-permute-done.24.refs_1_, ...), custom_call_target="tpu_custom_call" | custom-call | tf_op jit(solution)/shard_map/mix_channels/pallas_call | solution.py:556
  227.4 5.0 %mix_channels.4 = (bf16[2,4,16,1024]{3,2,1,0:T(8,128)(2,1)S(1)}, bf16[2,4,16,1024]{3,2,1,0:T(8,128)(2,1)S(1)}, bf16[2,4,16,1024]{3,2,1,0:T(8,128)(2,1)S(1)}, bf16[2,4,16,1024]{3,2,1,0:T(8,128)(2,1)S(1)}) custom-call(s32[7]{0:T(128)S(1)} %copy-done.8, bf16[2,256,256]{2,1,0:T(8,128)(2,1)S(1)} %collective-permute-done.25.refs_0_, ...), custom_call_target="tpu_custom_call" | custom-call | tf_op jit(solution)/shard_map/mix_channels/pallas_call | solution.py:556
  234.6 4.9 %mix_channels.5 = (bf16[2,4,16,1024]{3,2,1,0:T(8,128)(2,1)S(1)}, bf16[2,4,16,1024]{3,2,1,0:T(8,128)(2,1)S(1)}, bf16[2,4,16,1024]{3,2,1,0:T(8,128)(2,1)S(1)}, bf16[2,4,16,1024]{3,2,1,0:T(8,128)(2,1)S(1)}) custom-call(s32[7]{0:T(128)S(1)} %copy-done.8, bf16[2,256,256]{2,1,0:T(8,128)(2,1)S(1)} %collective-permute-done.34.refs_0_, ...), custom_call_target="tpu_custom_call" | custom-call | tf_op jit(solution)/shard_map/mix_channels/pallas_call | solution.py:556
  243.8 4.5 %collective-permute-done.36 = bf16[2,4,16,1024]{3,2,1,0:T(8,128)(2,1)S(1)} collective-permute-done((bf16[2,4,16,1024]{3,2,1,0:T(8,128)(2,1)S(1)}, bf16[2,4,16,1024]{3,2,1,0:T(8,128)(2,1)S(1)}, u32[]{:S(2)}, u32[]{:S(2)}) %collective-permute-start.36) | collective-permute-done | bytes 262176 | tf_op jit(solution)/shard_map/ppermute | solution.py:173
  250.5 2.9 %collective-permute-done.37 = bf16[4,16,1024]{2,1,0:T(8,128)(2,1)S(1)} collective-permute-done((bf16[4,16,1024]{2,1,0:T(8,128)(2,1)S(1)}, bf16[4,16,1024]{2,1,0:T(8,128)(2,1)S(1)}, u32[]{:S(2)}, u32[]{:S(2)}) %collective-permute-start.37) | collective-permute-done | bytes 131104 | tf_op jit(solution)/shard_map/ppermute | solution.py:173
  253.9 4.1 %collective-permute-start.41 = (bf16[4,16,1024]{2,1,0:T(8,128)(2,1)S(1)}, bf16[4,16,1024]{2,1,0:T(8,128)(2,1)S(1)}, u32[]{:S(2)}, u32[]{:S(2)}) collective-permute-start(bf16[4,16,1024]{2,1,0:T(8,128)(2,1)S(1)} %pad_maximum_fusion.5), channel_id=1, source_target_pairs={{0,16},{4,20},{8,24},{12,28},{16,0},{20,4},{24,8},{28,12},{1,17},{... | collective-permute-start | bytes 393224 | tf_op jit(solution)/shard_map/ppermute | solution.py:168
  (189 shorter events, 52.1 us)
Async XLA Ops:
  0.0 13.3 %all-to-all-start = ((bf16[4,32,2048]{2,1,0:T(8,128)(2,1)}), bf16[4,32,2048]{2,1,0:T(8,128)(2,1)S(1)}, u32[]{:S(2)}, u32[]{:S(2)}) async-start(bf16[4,32,2048]{2,1,0:T(8,128)(2,1)} %bitcast.151), calls=%async_computation | async-start | bytes 1048576 | tf_op jit(solution)/shard_map/all_to_all | solution.py:659
  14.7 20.2 %all-to-all-start.1 = ((bf16[8,32,1024]{2,1,0:T(8,128)(2,1)}), bf16[8,32,1024]{2,1,0:T(8,128)(2,1)S(1)}, u32[]{:S(2)}, u32[]{:S(2)}) async-start(bf16[8,32,1024]{2,1,0:T(8,128)(2,1)} %bitcast.1), calls=%async_computation.1 | async-start | bytes 1048576 | tf_op jit(solution)/shard_map/all_to_all | solution.py:674
  44.3 33.9 %collective-permute-start = (bf16[4,560,256]{2,1,0:T(8,128)(2,1)}, bf16[4,560,256]{2,1,0:T(8,128)(2,1)S(1)}, u32[]{:S(2)}, u32[]{:S(2)}) collective-permute-start(bf16[4,560,256]{2,1,0:T(8,128)(2,1)} %get-tuple-element.47), channel_id=1, source_target_pairs={{0,4},{4,0},{8,12},{12,8},{16,20},{20,16},{24,28},{28,24},{1,5},{5... | collective-permute-start | bytes 3440648 | tf_op jit(solution)/shard_map/ppermute | solution.py:162
  44.3 14.5 %collective-permute-start.4 = (bf16[256,1024]{1,0:T(8,128)(2,1)}, bf16[256,1024]{1,0:T(8,128)(2,1)S(1)}, u32[]{:S(2)}, u32[]{:S(2)}) collective-permute-start(bf16[256,1024]{1,0:T(8,128)(2,1)} %bitcast.154), channel_id=1, source_target_pairs={{0,1},{1,0},{2,3},{3,2},{4,5},{5,4},{6,7},{7,6},{8,9},{9,8},{10,11... | collective-permute-start | bytes 1572872 | tf_op jit(solution)/shard_map/ppermute | solution.py:173
  45.8 14.2 %collective-permute-start.5 = (bf16[256,1024]{1,0:T(8,128)(2,1)}, bf16[256,1024]{1,0:T(8,128)(2,1)S(1)}, u32[]{:S(2)}, u32[]{:S(2)}) collective-permute-start(bf16[256,1024]{1,0:T(8,128)(2,1)} %bitcast.155), channel_id=1, source_target_pairs={{0,2},{1,3},{2,0},{3,1},{4,6},{5,7},{6,4},{7,5},{8,10},{9,11},{10,... | collective-permute-start | bytes 1572872 | tf_op jit(solution)/shard_map/ppermute | solution.py:173
  60.0 14.2 %collective-permute-start.6 = (bf16[256,1024]{1,0:T(8,128)(2,1)}, bf16[256,1024]{1,0:T(8,128)(2,1)S(1)}, u32[]{:S(2)}, u32[]{:S(2)}) collective-permute-start(bf16[256,1024]{1,0:T(8,128)(2,1)} %bitcast.156), channel_id=1, source_target_pairs={{0,3},{1,2},{2,1},{3,0},{4,7},{5,6},{6,5},{7,4},{8,11},{9,10},{10,... | collective-permute-start | bytes 1572872 | tf_op jit(solution)/shard_map/ppermute | solution.py:173
  78.1 11.5 %collective-permute-start.11 = (bf16[4,400,256]{2,1,0:T(8,128)(2,1)S(1)}, bf16[4,400,256]{2,1,0:T(8,128)(2,1)S(1)}, u32[]{:S(2)}, u32[]{:S(2)}) collective-permute-start(bf16[4,400,256]{2,1,0:T(8,128)(2,1)S(1)} %get-tuple-element.55), channel_id=1, source_target_pairs={{0,4},{4,0},{8,12},{12,8},{16,20},{20,16},{24,28},{28,24},{1,5},{5... | collective-permute-start | bytes 2457608 | tf_op jit(solution)/shard_map/ppermute | solution.py:162
  78.3 11.1 %collective-permute-start.1 = (bf16[560,256]{1,0:T(8,128)(2,1)S(1)}, bf16[560,256]{1,0:T(8,128)(2,1)S(1)}, u32[]{:S(2)}, u32[]{:S(2)}) collective-permute-start(bf16[560,256]{1,0:T(8,128)(2,1)S(1)} %fusion.12), channel_id=1, source_target_pairs={{0,8},{4,12},{8,16},{12,20},{16,24},{20,28},{24,0},{28,4},{1,9},{5... | collective-permute-start | bytes 860168 | tf_op jit(solution)/shard_map/ppermute | solution.py:168
  83.3 31.6 %collective-permute-start.7 = (bf16[4,768,256]{2,1,0:T(8,128)(2,1)S(1)}, bf16[4,768,256]{2,1,0:T(8,128)(2,1)S(1)}, u32[]{:S(2)}, u32[]{:S(2)}) collective-permute-start(bf16[4,768,256]{2,1,0:T(8,128)(2,1)S(1)} %get-tuple-element.52), channel_id=1, source_target_pairs={{0,4},{4,0},{8,12},{12,8},{16,20},{20,16},{24,28},{28,24},{1,5},{5... | collective-permute-start | bytes 4718600 | tf_op jit(solution)/shard_map/ppermute | solution.py:162
  89.4 11.6 %collective-permute-start.2 = (bf16[560,256]{1,0:T(8,128)(2,1)S(1)}, bf16[560,256]{1,0:T(8,128)(2,1)S(1)}, u32[]{:S(2)}, u32[]{:S(2)}) collective-permute-start(bf16[560,256]{1,0:T(8,128)(2,1)S(1)} %fusion.5), channel_id=1, source_target_pairs={{0,8},{4,12},{8,16},{12,20},{16,24},{20,28},{24,0},{28,4},{1,9},{5... | collective-permute-start | bytes 860168 | tf_op jit(solution)/shard_map/ppermute | solution.py:168
  89.5 132.1 %collective-permute-start.27 = (bf16[2048,1024]{1,0:T(8,128)(2,1)}, bf16[2048,1024]{1,0:T(8,128)(2,1)}, u32[]{:S(2)}, u32[]{:S(2)}) collective-permute-start(bf16[2048,1024]{1,0:T(8,128)(2,1)} %refs_3_.7), channel_id=1, source_target_pairs={{0,4},{4,0},{8,12},{12,8},{16,20},{20,16},{24,28},{28,24},{1,5},{5... | collective-permute-start | bytes 12582920 | tf_op jit(solution)/shard_map/ppermute | solution.py:162
  89.7 15.4 %collective-permute-start.12 = (bf16[400,256]{1,0:T(8,128)(2,1)S(1)}, bf16[400,256]{1,0:T(8,128)(2,1)S(1)}, u32[]{:S(2)}, u32[]{:S(2)}) collective-permute-start(bf16[400,256]{1,0:T(8,128)(2,1)S(1)} %fusion.14), channel_id=1, source_target_pairs={{0,8},{4,12},{8,16},{12,20},{16,24},{20,28},{24,0},{28,4},{1,9},{5... | collective-permute-start | bytes 614408 | tf_op jit(solution)/shard_map/ppermute | solution.py:168
  105.0 19.8 %collective-permute-start.15 = (bf16[4,512,256]{2,1,0:T(8,128)(2,1)S(1)}, bf16[4,512,256]{2,1,0:T(8,128)(2,1)S(1)}, u32[]{:S(2)}, u32[]{:S(2)}) collective-permute-start(bf16[4,512,256]{2,1,0:T(8,128)(2,1)S(1)} %get-tuple-element.57), channel_id=1, source_target_pairs={{0,4},{4,0},{8,12},{12,8},{16,20},{20,16},{24,28},{28,24},{1,5},{5... | collective-permute-start | bytes 3145736 | tf_op jit(solution)/shard_map/ppermute | solution.py:162
  105.2 9.6 %collective-permute-start.13 = (bf16[400,256]{1,0:T(8,128)(2,1)S(1)}, bf16[400,256]{1,0:T(8,128)(2,1)S(1)}, u32[]{:S(2)}, u32[]{:S(2)}) collective-permute-start(bf16[400,256]{1,0:T(8,128)(2,1)S(1)} %fusion.9), channel_id=1, source_target_pairs={{0,8},{4,12},{8,16},{12,20},{16,24},{20,28},{24,0},{28,4},{1,9},{5... | collective-permute-start | bytes 614408 | tf_op jit(solution)/shard_map/ppermute | solution.py:168
  114.9 9.8 %collective-permute-start.14 = (bf16[400,256]{1,0:T(8,128)(2,1)S(1)}, bf16[400,256]{1,0:T(8,128)(2,1)S(1)}, u32[]{:S(2)}, u32[]{:S(2)}) collective-permute-start(bf16[400,256]{1,0:T(8,128)(2,1)S(1)} %fusion.10), channel_id=1, source_target_pairs={{0,8},{4,12},{8,16},{12,20},{16,24},{20,28},{24,0},{28,4},{1,9},{5... | collective-permute-start | bytes 614408 | tf_op jit(solution)/shard_map/ppermute | solution.py:168
  115.1 20.1 %collective-permute-start.8 = (bf16[768,256]{1,0:T(8,128)(2,1)S(1)}, bf16[768,256]{1,0:T(8,128)(2,1)S(1)}, u32[]{:S(2)}, u32[]{:S(2)}) collective-permute-start(bf16[768,256]{1,0:T(8,128)(2,1)S(1)} %fusion.11), channel_id=1, source_target_pairs={{0,8},{4,12},{8,16},{12,20},{16,24},{20,28},{24,0},{28,4},{1,9},{5... | collective-permute-start | bytes 1179656 | tf_op jit(solution)/shard_map/ppermute | solution.py:168
  124.8 10.5 %collective-permute-start.19 = (bf16[192,256]{1,0:T(8,128)(2,1)S(1)}, bf16[192,256]{1,0:T(8,128)(2,1)S(1)}, u32[]{:S(2)}, u32[]{:S(2)}) collective-permute-start(bf16[192,256]{1,0:T(8,128)(2,1)S(1)} %get-tuple-element.102), channel_id=1, source_target_pairs={{0,8},{4,12},{8,16},{12,20},{16,24},{20,28},{24,0},{28,4},{1,9},{5... | collective-permute-start | bytes 294920 | tf_op jit(solution)/shard_map/ppermute | solution.py:168
  124.9 18.0 %collective-permute-start.16 = (bf16[512,256]{1,0:T(8,128)(2,1)S(1)}, bf16[512,256]{1,0:T(8,128)(2,1)S(1)}, u32[]{:S(2)}, u32[]{:S(2)}) collective-permute-start(bf16[512,256]{1,0:T(8,128)(2,1)S(1)} %fusion.13), channel_id=1, source_target_pairs={{0,8},{4,12},{8,16},{12,20},{16,24},{20,28},{24,0},{28,4},{1,9},{5... | collective-permute-start | bytes 786440 | tf_op jit(solution)/shard_map/ppermute | solution.py:168
  135.4 18.3 %collective-permute-start.9 = (bf16[768,256]{1,0:T(8,128)(2,1)S(1)}, bf16[768,256]{1,0:T(8,128)(2,1)S(1)}, u32[]{:S(2)}, u32[]{:S(2)}) collective-permute-start(bf16[768,256]{1,0:T(8,128)(2,1)S(1)} %fusion.3), channel_id=1, source_target_pairs={{0,8},{4,12},{8,16},{12,20},{16,24},{20,28},{24,0},{28,4},{1,9},{5... | collective-permute-start | bytes 1179656 | tf_op jit(solution)/shard_map/ppermute | solution.py:168
  142.9 10.5 %collective-permute-start.21 = (bf16[192,256]{1,0:T(8,128)(2,1)S(1)}, bf16[192,256]{1,0:T(8,128)(2,1)S(1)}, u32[]{:S(2)}, u32[]{:S(2)}) collective-permute-start(bf16[192,256]{1,0:T(8,128)(2,1)S(1)} %collective-permute-done.20), channel_id=1, source_target_pairs={{0,8},{4,12},{8,16},{12,20},{16,24},{20,28},{24,0},{28,4},{1,9},{5... | collective-permute-start | bytes 294920 | tf_op jit(solution)/shard_map/ppermute | solution.py:168
  143.1 15.0 %collective-permute-start.17 = (bf16[512,256]{1,0:T(8,128)(2,1)S(1)}, bf16[512,256]{1,0:T(8,128)(2,1)S(1)}, u32[]{:S(2)}, u32[]{:S(2)}) collective-permute-start(bf16[512,256]{1,0:T(8,128)(2,1)S(1)} %fusion.7), channel_id=1, source_target_pairs={{0,8},{4,12},{8,16},{12,20},{16,24},{20,28},{24,0},{28,4},{1,9},{5... | collective-permute-start | bytes 786440 | tf_op jit(solution)/shard_map/ppermute | solution.py:168
  153.5 19.2 %collective-permute-start.22 = (bf16[4,192,256]{2,1,0:T(8,128)(2,1)S(1)}, bf16[4,192,256]{2,1,0:T(8,128)(2,1)S(1)}, u32[]{:S(2)}, u32[]{:S(2)}) collective-permute-start(bf16[4,192,256]{2,1,0:T(8,128)(2,1)S(1)} %pad_maximum_fusion.1.refs_9_), channel_id=1, source_target_pairs={{0,4},{4,0},{8,12},{12,8},{16,20},{20,16},{24,28},{28,24},{1,5},{5... | collective-permute-start | bytes 1179656 | tf_op jit(solution)/shard_map/ppermute | solution.py:162
  153.8 32.9 %collective-permute-start.10 = (bf16[768,256]{1,0:T(8,128)(2,1)S(1)}, bf16[768,256]{1,0:T(8,128)(2,1)S(1)}, u32[]{:S(2)}, u32[]{:S(2)}) collective-permute-start(bf16[768,256]{1,0:T(8,128)(2,1)S(1)} %fusion.4), channel_id=1, source_target_pairs={{0,8},{4,12},{8,16},{12,20},{16,24},{20,28},{24,0},{28,4},{1,9},{5... | collective-permute-start | bytes 1179656 | tf_op jit(solution)/shard_map/ppermute | solution.py:168
  158.1 14.6 %collective-permute-start.18 = (bf16[512,256]{1,0:T(8,128)(2,1)S(1)}, bf16[512,256]{1,0:T(8,128)(2,1)S(1)}, u32[]{:S(2)}, u32[]{:S(2)}) collective-permute-start(bf16[512,256]{1,0:T(8,128)(2,1)S(1)} %fusion.8), channel_id=1, source_target_pairs={{0,8},{4,12},{8,16},{12,20},{16,24},{20,28},{24,0},{28,4},{1,9},{5... | collective-permute-start | bytes 786440 | tf_op jit(solution)/shard_map/ppermute | solution.py:168
  193.7 11.0 %collective-permute-start.24 = (bf16[2,256,256]{2,1,0:T(8,128)(2,1)S(1)}, bf16[2,256,256]{2,1,0:T(8,128)(2,1)S(1)}, u32[]{:S(2)}, u32[]{:S(2)}) collective-permute-start(bf16[2,256,256]{2,1,0:T(8,128)(2,1)S(1)} %pad_maximum_fusion.2.refs_0_), channel_id=1, source_target_pairs={{0,8},{4,12},{8,16},{12,20},{16,24},{20,28},{24,0},{28,4},{1,9},{5... | collective-permute-start | bytes 786440 | tf_op jit(solution)/shard_map/ppermute | solution.py:168
  196.3 14.1 %collective-permute-start.29 = (bf16[2,256,256]{2,1,0:T(8,128)(2,1)S(1)}, bf16[2,256,256]{2,1,0:T(8,128)(2,1)}, u32[]{:S(2)}, u32[]{:S(2)}) collective-permute-start(bf16[2,256,256]{2,1,0:T(8,128)(2,1)S(1)} %pad_maximum_fusion.3.refs_2_), channel_id=1, source_target_pairs={{0,8},{4,12},{8,16},{12,20},{16,24},{20,28},{24,0},{28,4},{1,9},{5... | collective-permute-start | bytes 786440 | tf_op jit(solution)/shard_map/ppermute | solution.py:168
  204.7 11.2 %collective-permute-start.25 = (bf16[2,256,256]{2,1,0:T(8,128)(2,1)S(1)}, bf16[2,256,256]{2,1,0:T(8,128)(2,1)S(1)}, u32[]{:S(2)}, u32[]{:S(2)}) collective-permute-start(bf16[2,256,256]{2,1,0:T(8,128)(2,1)S(1)} %collective-permute-done.24.refs_1_), channel_id=1, source_target_pairs={{0,8},{4,12},{8,16},{12,20},{16,24},{20,28},{24,0},{28,4},{1,9},{5... | collective-permute-start | bytes 786440 | tf_op jit(solution)/shard_map/ppermute | solution.py:168
  210.5 11.2 %collective-permute-start.34 = (bf16[2,256,256]{2,1,0:T(8,128)(2,1)}, bf16[2,256,256]{2,1,0:T(8,128)(2,1)S(1)}, u32[]{:S(2)}, u32[]{:S(2)}) collective-permute-start(bf16[2,256,256]{2,1,0:T(8,128)(2,1)} %collective-permute-done.29.refs_3_), channel_id=1, source_target_pairs={{0,8},{4,12},{8,16},{12,20},{16,24},{20,28},{24,0},{28,4},{1,9},{5... | collective-permute-start | bytes 786440 | tf_op jit(solution)/shard_map/ppermute | solution.py:168
  216.0 11.4 %collective-permute-start.26 = (bf16[2,256,256]{2,1,0:T(8,128)(2,1)S(1)}, bf16[2,256,256]{2,1,0:T(8,128)(2,1)}, u32[]{:S(2)}, u32[]{:S(2)}) collective-permute-start(bf16[2,256,256]{2,1,0:T(8,128)(2,1)S(1)} %collective-permute-done.25.refs_0_), channel_id=1, source_target_pairs={{0,8},{4,12},{8,16},{12,20},{16,24},{20,28},{24,0},{28,4},{1,9},{5... | collective-permute-start | bytes 786440 | tf_op jit(solution)/shard_map/ppermute | solution.py:168
  221.7 13.0 %collective-permute-start.35 = (bf16[2,256,256]{2,1,0:T(8,128)(2,1)S(1)}, bf16[2,256,256]{2,1,0:T(8,128)(2,1)S(1)}, u32[]{:S(2)}, u32[]{:S(2)}) collective-permute-start(bf16[2,256,256]{2,1,0:T(8,128)(2,1)S(1)} %collective-permute-done.34.refs_0_), channel_id=1, source_target_pairs={{0,8},{4,12},{8,16},{12,20},{16,24},{20,28},{24,0},{28,4},{1,9},{5... | collective-permute-start | bytes 786440 | tf_op jit(solution)/shard_map/ppermute | solution.py:168
  233.1 9.1 %collective-permute-start.32 = (bf16[2,4,16,1024]{3,2,1,0:T(8,128)(2,1)S(1)}, bf16[2,4,16,1024]{3,2,1,0:T(8,128)(2,1)S(1)}, u32[]{:S(2)}, u32[]{:S(2)}) collective-permute-start(bf16[2,4,16,1024]{3,2,1,0:T(8,128)(2,1)S(1)} %get-tuple-element.72), channel_id=1, source_target_pairs={{0,2},{1,3},{2,0},{3,1},{4,6},{5,7},{6,4},{7,5},{8,10},{9,11},{10,... | collective-permute-start | bytes 786440 | tf_op jit(solution)/shard_map/ppermute | solution.py:173
  253.9 9.6 %collective-permute-start.41 = (bf16[4,16,1024]{2,1,0:T(8,128)(2,1)S(1)}, bf16[4,16,1024]{2,1,0:T(8,128)(2,1)S(1)}, u32[]{:S(2)}, u32[]{:S(2)}) collective-permute-start(bf16[4,16,1024]{2,1,0:T(8,128)(2,1)S(1)} %pad_maximum_fusion.5), channel_id=1, source_target_pairs={{0,16},{4,20},{8,24},{12,28},{16,0},{20,4},{24,8},{28,12},{1,17},{... | collective-permute-start | bytes 393224 | tf_op jit(solution)/shard_map/ppermute | solution.py:168
  (44 other events, 745.3 us)

commit v2 on v1

--- a/solution.py
+++ b/solution.py
@@ -307,7 +307,7 @@
                     )
             return carry
 
-        lax.fori_loop(0, stretches, place_rows, 0)
+        lax.fori_loop(0, stretches, place_rows, 0, unroll=2)
         for source, own_core in ((thin_ref, core), (swapped_ref, 1 - core)):
             for away in range(chips):
                 stretch = own_core * chips + lax.rem(chip + chips - away, chips)
@@ -399,7 +399,7 @@
             )
             return carry
 
-        lax.fori_loop(0, stretches, chunk, 0)
+        lax.fori_loop(0, stretches, chunk, 0, unroll=4)
 
     whole = lambda value: pl.BlockSpec(value.shape, lambda i, order, starts: (0,) * value.ndim)
     trio_specs = [
@@ -461,7 +461,7 @@
                             ]
             return carry
 
-        lax.fori_loop(0, chips, one_chip, 0)
+        lax.fori_loop(0, chips, one_chip, 0, unroll=2)
 
     whole = lambda shape: pl.BlockSpec(shape, lambda i, order: (0,) * len(shape))
     shape = (chips, quarters, half, width)
@@ -483,7 +483,7 @@
     )(order, *flat, outputs.reshape(stretches, quarters, rows, width))
 
 
-def mix_channels(order, pairs, away, so_far, gains, own_proj, other_proj, sizes):
+def mix_channels(order, pairs, away, so_far, gains, own_proj, other_proj, sizes, grant):
     stretches, rows, quarters, width = sizes
     half, chips = rows // 2, stretches // 2
     count = pairs[0].shape[1]
@@ -565,7 +565,7 @@
             out_specs=[whole(value.shape) for value in outs],
             scratch_shapes=scratch if last else [],
         ),
-        compiler_params=pltpu.CompilerParams(vmem_limit_bytes=VMEM_BYTES),
+        compiler_params=pltpu.CompilerParams(vmem_limit_bytes=grant),
         name="mix_channels",
     )(order, *pairs, gains, own_proj, other_proj, *so_far)
 
@@ -679,8 +679,10 @@
     )
 
     near = [flip_fsdp(own, 1), flip_fsdp(own, 2)]
-    near[0], near[1], again = lax.optimization_barrier((near[0], near[1], own))
-    pieces = [own, *near, flip_fsdp(again, 3)]
+    middle = own.shape[0] // 2
+    upper = flip_fsdp(near[1][:middle], 1)
+    lower = flip_fsdp(near[0][middle:], 2)
+    pieces = [own, *near, jnp.concatenate([upper, lower], axis=0)]
 
     def reduced(members, projections, plan, thin_places=(), grant=VMEM_BYTES):
         lent, kept = share_partials(
@@ -724,12 +726,13 @@
             blocks.append(next_chip(blocks[-1]))
         shares.append(blocks)
     so_far = mix_channels(
-        order, shares[0][:2] + shares[1][:2], 0, None, gains, out_proj, other_proj, sizes
+        order, shares[0][:2] + shares[1][:2], 0, None, gains, out_proj, other_proj, sizes,
+        VMEM_BYTES,
     )
     for part in range(2):
         left_kept, left_sent, right_kept, right_sent = mix_channels(
             order, shares[part][2:], 2, so_far[2 * part : 2 * part + 2], gains, out_proj,
-            other_proj, sizes,
+            other_proj, sizes, VMEM_BYTES,
         )
         left_got = flip_fsdp(left_sent, 1)
         right_got = flip_fsdp(right_sent, 2)

time: 275 us -> 268 us (0.975)
  waiting for transfers between devices: 169 us -> 162 us
    ppermute x14 -> x15, waiting for transfers between devices: 38.8 us -> 31.8 us  [flip_fsdp(): lax.ppermute(value, 'fsdp', [(place, place ^ bits) for place in range(cou...]
    ppermute x14 -> x15, starting transfers between devices: 15.4 us -> 16 us  [flip_fsdp(): lax.ppermute(value, 'fsdp', [(place, place ^ bits) for place in range(cou...]
  transfers between devices with their start and end apart: 48 -> 49, of which waited for: 31 -> 31; matrix products, arithmetic and copies ran while one was open for 5% -> 5% of each run, Pallas kernels for 16% -> 16%
where the time goes in v2:
time: 268 us; the launch traced here: 267 us
  waiting for transfers between devices  162 us (60%)
  Pallas kernels  53.8 us (20%)
  starting transfers between devices  33 us (12%)
  local copies, waits for them, and re-layouts  10.2 us (4%)
  other arithmetic  7.3 us (3%)
    ppermute x24, waiting for transfers between devices, next_chip(): return lax.ppermute(value, 'seq', route)  114 us
    ppermute x15, waiting for transfers between devices, flip_fsdp(): lax.ppermute(value, 'fsdp', [(place, place ^ bits) for place in range(cou...  31.8 us
    pallas_call x4, Pallas kernels, share_partials(): pl.pallas_call(body, out_shape=[out, out], grid_spec=pltpu.PrefetchScalar...  21.1 us
    ppermute x15, starting transfers between devices, flip_fsdp(): lax.ppermute(value, 'fsdp', [(place, place ^ bits) for place in range(cou...  16 us
    pallas_call x3, Pallas kernels, mix_channels(): pl.pallas_call(body, out_shape=outs, grid_spec=pltpu.PrefetchScalarGridSp...  15.6 us
    pallas_call x1, Pallas kernels, scan_heads(): pl.pallas_call(body, out_shape=jax.ShapeDtypeStruct((tokens, width), jnp....  11.9 us
    all_to_all x1, waiting for transfers between devices, by_channel(): lax.all_to_all(tokens.reshape(quarters, rows, features), 'fsdp', split_ax...  7.24 us
    all_to_all x1, waiting for transfers between devices, by_channel(): lax.all_to_all(slices, 'seq', split_axis=0, concat_axis=0, tiled=True)  6.7 us
  transfers between devices with their start and end apart: 49, of which 31 were waited for; matrix products, arithmetic and copies ran while one was open for 5% of the time, Pallas kernels for 16%

profile of v2, /device:TPU:0, one launch (start us, length us, event | category | flops | bytes accessed | tf_op | source)
XLA Modules:
  0.0 267.5 jit_solution(11997274608665126884)
XLA Ops:
  0.0 5.3 %all-to-all-start = ((bf16[4,32,2048]{2,1,0:T(8,128)(2,1)}), bf16[4,32,2048]{2,1,0:T(8,128)(2,1)S(1)}, u32[]{:S(2)}, u32[]{:S(2)}) async-start(bf16[4,32,2048]{2,1,0:T(8,128)(2,1)} %bitcast.151), calls=%async_computation | async-start | bytes 1048576 | tf_op jit(solution)/shard_map/all_to_all | solution.py:659
  6.1 7.2 %all-to-all-done = bf16[4,32,2048]{2,1,0:T(8,128)(2,1)S(1)} async-done(((bf16[4,32,2048]{2,1,0:T(8,128)(2,1)}), bf16[4,32,2048]{2,1,0:T(8,128)(2,1)S(1)}, u32[]{:S(2)}, u32[]{:S(2)}) %all-to-all-start) | async-done | bytes 524320 | tf_op jit(solution)/shard_map/all_to_all | solution.py:659
  14.7 4.9 %all-to-all-start.1 = ((bf16[8,32,1024]{2,1,0:T(8,128)(2,1)}), bf16[8,32,1024]{2,1,0:T(8,128)(2,1)S(1)}, u32[]{:S(2)}, u32[]{:S(2)}) async-start(bf16[8,32,1024]{2,1,0:T(8,128)(2,1)} %bitcast.1), calls=%async_computation.1 | async-start | bytes 1048576 | tf_op jit(solution)/shard_map/all_to_all | solution.py:674
  28.2 6.7 %all-to-all-done.1 = bf16[8,32,1024]{2,1,0:T(8,128)(2,1)S(1)} async-done(((bf16[8,32,1024]{2,1,0:T(8,128)(2,1)}), bf16[8,32,1024]{2,1,0:T(8,128)(2,1)S(1)}, u32[]{:S(2)}, u32[]{:S(2)}) %all-to-all-start.1) | async-done | bytes 524320 | tf_op jit(solution)/shard_map/all_to_all | solution.py:674
  35.7 8.6 %share_partials.4 = (bf16[4,560,256]{2,1,0:T(8,128)(2,1)}, bf16[4,560,256]{2,1,0:T(8,128)(2,1)}) custom-call(s32[2]{0:T(128)} %pad_add_fusion.where, bf16[256,1024]{1,0:T(8,128)(2,1)} %bitcast.153, bf16[1024,2048]{1,0:T(8,128)(2,1)} %refs_2_.3, bf16[1024,2048]{1,0:T(8,128)(2,1)} %refs_3_.4, bf16[1024,384]{1,0:T(8,128)(2,1)} %maximum_maximum_fusion.refs_3_.refs_4_), custom_call_target="tpu_custom_call" | custom-call | tf_op jit(solution)/shard_map/share_partials/pallas_call | solution.py:229
  46.4 12.5 %collective-permute-done.5.refs_1_.refs_2_ = bf16[256,1024]{1,0:T(8,128)(2,1)S(1)} collective-permute-done((bf16[256,1024]{1,0:T(8,128)(2,1)}, bf16[256,1024]{1,0:T(8,128)(2,1)S(1)}, u32[]{:S(2)}, u32[]{:S(2)}) %collective-permute-start.5) | collective-permute-done | bytes 524320 | tf_op jit(solution)/shard_map/ppermute | solution.py:173
  61.1 5.7 %collective-permute-done.6 = bf16[128,1024]{1,0:T(8,128)(2,1)S(1)} collective-permute-done((bf16[128,1024]{1,0:T(8,128)(2,1)S(1)}, bf16[128,1024]{1,0:T(8,128)(2,1)S(1)}, u32[]{:S(2)}, u32[]{:S(2)}) %collective-permute-start.6) | collective-permute-done | bytes 262176 | tf_op jit(solution)/shard_map/ppermute | solution.py:173
  68.1 3.8 %share_partials.6 = (bf16[4,400,256]{2,1,0:T(8,128)(2,1)S(1)}, bf16[4,400,256]{2,1,0:T(8,128)(2,1)S(1)}) custom-call(s32[2]{0:T(128)S(1)} %copy-done.9, bf16[256,1024]{1,0:T(8,128)(2,1)S(1)} %constant_dynamic-update-slice_fusion.refs_2_.refs_0_, bf16[256,1024]{1,0:T(8,128)(2,1)S(1)} %collective-permute-done.4.refs_0_.refs_1_, ...), custom_call_target="tpu_custom_call" | custom-call | tf_op jit(solution)/shard_map/share_partials/pallas_call | solution.py:229
  72.1 4.9 %share_partials.5 = (bf16[4,768,256]{2,1,0:T(8,128)(2,1)S(1)}, bf16[4,768,256]{2,1,0:T(8,128)(2,1)S(1)}) custom-call(s32[2]{0:T(128)S(1)} %copy-done.9, bf16[256,1024]{1,0:T(8,128)(2,1)S(1)} %collective-permute-done.4.refs_0_.refs_1_, bf16[256,1024]{1,0:T(8,128)(2,1)S(1)} %collective-permute-done.5.refs_1_.refs_2_, ...), custom_call_target="tpu_custom_call" | custom-call | tf_op jit(solution)/shard_map/share_partials/pallas_call | solution.py:229
  77.6 5.5 %collective-permute-done.1 = bf16[560,256]{1,0:T(8,128)(2,1)S(1)} collective-permute-done((bf16[560,256]{1,0:T(8,128)(2,1)S(1)}, bf16[560,256]{1,0:T(8,128)(2,1)S(1)}, u32[]{:S(2)}, u32[]{:S(2)}) %collective-permute-start.1) | collective-permute-done | bytes 286752 | tf_op jit(solution)/shard_map/ppermute | solution.py:168
  83.5 11.3 %collective-permute-done.2 = bf16[560,256]{1,0:T(8,128)(2,1)S(1)} collective-permute-done((bf16[560,256]{1,0:T(8,128)(2,1)S(1)}, bf16[560,256]{1,0:T(8,128)(2,1)S(1)}, u32[]{:S(2)}, u32[]{:S(2)}) %collective-permute-start.2) | collective-permute-done | bytes 286752 | tf_op jit(solution)/shard_map/ppermute | solution.py:168
  95.0 3.8 %share_partials.7 = (bf16[4,512,256]{2,1,0:T(8,128)(2,1)S(1)}, bf16[4,512,256]{2,1,0:T(8,128)(2,1)S(1)}) custom-call(s32[2]{0:T(128)S(1)} %copy-done.9, bf16[256,1024]{1,0:T(8,128)(2,1)S(1)} %collective-permute-done.4.refs_0_.refs_1_, bf16[256,1024]{1,0:T(8,128)(2,1)S(1)} %collective-permute-done.5.refs_1_.refs_2_, bf16[1024,2048]{1,0:T(8,128)(2,1)S(1)} %copy-done.1), custom_call_target="tpu_custom_call" | custom-call | tf_op jit(solution)/shard_map/share_partials/pallas_call | solution.py:229
  99.1 4.9 %collective-permute-done.3.refs_2_ = bf16[560,256]{1,0:T(8,128)(2,1)S(1)} collective-permute-done((bf16[560,256]{1,0:T(8,128)(2,1)S(1)}, bf16[560,256]{1,0:T(8,128)(2,1)S(1)}, u32[]{:S(2)}, u32[]{:S(2)}) %collective-permute-start.3) | collective-permute-done | bytes 286752 | tf_op jit(solution)/shard_map/ppermute | solution.py:168
  104.0 4.6 %collective-permute-done.14 = bf16[400,256]{1,0:T(8,128)(2,1)S(1)} collective-permute-done((bf16[400,256]{1,0:T(8,128)(2,1)S(1)}, bf16[400,256]{1,0:T(8,128)(2,1)S(1)}, u32[]{:S(2)}, u32[]{:S(2)}) %collective-permute-start.14) | collective-permute-done | bytes 204832 | tf_op jit(solution)/shard_map/ppermute | solution.py:168
  109.3 9.2 %collective-permute-done.15.refs_5_ = bf16[400,256]{1,0:T(8,128)(2,1)S(1)} collective-permute-done((bf16[400,256]{1,0:T(8,128)(2,1)S(1)}, bf16[400,256]{1,0:T(8,128)(2,1)S(1)}, u32[]{:S(2)}, u32[]{:S(2)}) %collective-permute-start.15) | collective-permute-done | bytes 204832 | tf_op jit(solution)/shard_map/ppermute | solution.py:168
  118.8 10.2 %collective-permute-done.20 = bf16[192,256]{1,0:T(8,128)(2,1)S(1)} collective-permute-done((bf16[192,256]{1,0:T(8,128)(2,1)S(1)}, bf16[192,256]{1,0:T(8,128)(2,1)S(1)}, u32[]{:S(2)}, u32[]{:S(2)}) %collective-permute-start.20) | collective-permute-done | bytes 98336 | tf_op jit(solution)/shard_map/ppermute | solution.py:168
  129.3 7.5 %collective-permute-done.21 = bf16[192,256]{1,0:T(8,128)(2,1)S(1)} collective-permute-done((bf16[192,256]{1,0:T(8,128)(2,1)S(1)}, bf16[192,256]{1,0:T(8,128)(2,1)S(1)}, u32[]{:S(2)}, u32[]{:S(2)}) %collective-permute-start.21) | collective-permute-done | bytes 98336 | tf_op jit(solution)/shard_map/ppermute | solution.py:168
  137.0 10.3 %collective-permute-done.22 = bf16[192,256]{1,0:T(8,128)(2,1)S(1)} collective-permute-done((bf16[192,256]{1,0:T(8,128)(2,1)S(1)}, bf16[192,256]{1,0:T(8,128)(2,1)S(1)}, u32[]{:S(2)}, u32[]{:S(2)}) %collective-permute-start.22) | collective-permute-done | bytes 98336 | tf_op jit(solution)/shard_map/ppermute | solution.py:168
  147.7 4.2 %collective-permute-done.18 = bf16[512,256]{1,0:T(8,128)(2,1)S(1)} collective-permute-done((bf16[512,256]{1,0:T(8,128)(2,1)S(1)}, bf16[512,256]{1,0:T(8,128)(2,1)S(1)}, u32[]{:S(2)}, u32[]{:S(2)}) %collective-permute-start.18) | collective-permute-done | bytes 262176 | tf_op jit(solution)/shard_map/ppermute | solution.py:168
  152.2 14.4 %collective-permute-done.19.refs_8_ = bf16[512,256]{1,0:T(8,128)(2,1)S(1)} collective-permute-done((bf16[512,256]{1,0:T(8,128)(2,1)S(1)}, bf16[512,256]{1,0:T(8,128)(2,1)S(1)}, u32[]{:S(2)}, u32[]{:S(2)}) %collective-permute-start.19) | collective-permute-done | bytes 262176 | tf_op jit(solution)/shard_map/ppermute | solution.py:168
  168.1 11.9 %scan_heads.1 = f32[1024,256]{1,0:T(8,128)} custom-call(s32[7]{0:T(128)} %stack.85.order, s32[16]{0:T(128)} %sub.19.starts_ref, bf16[4,560,256]{2,1,0:T(8,128)(2,1)} %get-tuple-element.43.refs_0_, bf16[4,560,256]{2,1,0:T(8,128)(2,1)} %copy-done.11, bf16[560,256]{1,0:T(8,128)(2,1)} %copy-done.17, bf16[4,400,256]{2,1,0:T(8,128)(2,1)} %copy-done.6, ...), custom_call_target="tpu_custom_call" | custom-call | tf_op jit(solution)/shard_map/scan_heads/pallas_call | solution.py:412
  180.7 3.8 %gate_outputs.1 = (bf16[4,4,16,256]{3,2,1,0:T(8,128)(2,1)}, bf16[4,4,16,256]{3,2,1,0:T(8,128)(2,1)}, bf16[4,4,16,256]{3,2,1,0:T(8,128)(2,1)}, bf16[4,4,16,256]{3,2,1,0:T(8,128)(2,1)}) custom-call(s32[7]{0:T(128)} %stack.85.order, bf16[4,560,256]{2,1,0:T(8,128)(2,1)} %get-tuple-element.43.refs_0_, bf16[4,560,256]{2,1,0:T(8,128)(2,1)} %copy-done.11, ...), custom_call_target="tpu_custom_call" | custom-call | tf_op jit(solution)/shard_map/gate_outputs/pallas_call | solution.py:468
  189.7 8.3 %collective-permute-done.25.refs_1_ = bf16[2,256,256]{2,1,0:T(8,128)(2,1)S(1)} collective-permute-done((bf16[2,256,256]{2,1,0:T(8,128)(2,1)S(1)}, bf16[2,256,256]{2,1,0:T(8,128)(2,1)S(1)}, u32[]{:S(2)}, u32[]{:S(2)}) %collective-permute-start.25) | collective-permute-done | bytes 262176 | tf_op jit(solution)/shard_map/ppermute | solution.py:168
  198.0 5.7 %collective-permute-done.30.refs_3_ = bf16[2,256,256]{2,1,0:T(8,128)(2,1)} collective-permute-done((bf16[2,256,256]{2,1,0:T(8,128)(2,1)S(1)}, bf16[2,256,256]{2,1,0:T(8,128)(2,1)}, u32[]{:S(2)}, u32[]{:S(2)}) %collective-permute-start.30) | collective-permute-done | bytes 262176 | tf_op jit(solution)/shard_map/ppermute | solution.py:168
  203.8 5.5 %collective-permute-done.26.refs_0_ = bf16[2,256,256]{2,1,0:T(8,128)(2,1)S(1)} collective-permute-done((bf16[2,256,256]{2,1,0:T(8,128)(2,1)S(1)}, bf16[2,256,256]{2,1,0:T(8,128)(2,1)S(1)}, u32[]{:S(2)}, u32[]{:S(2)}) %collective-permute-start.26) | collective-permute-done | bytes 262176 | tf_op jit(solution)/shard_map/ppermute | solution.py:168
  209.3 5.7 %collective-permute-done.35.refs_0_ = bf16[2,256,256]{2,1,0:T(8,128)(2,1)S(1)} collective-permute-done((bf16[2,256,256]{2,1,0:T(8,128)(2,1)}, bf16[2,256,256]{2,1,0:T(8,128)(2,1)S(1)}, u32[]{:S(2)}, u32[]{:S(2)}) %collective-permute-start.35) | collective-permute-done | bytes 262176 | tf_op jit(solution)/shard_map/ppermute | solution.py:168
  214.9 5.7 %mix_channels.3 = (f32[256,2048]{1,0:T(8,128)S(1)}, f32[256,128]{1,0:T(8,128)S(1)}, f32[256,2048]{1,0:T(8,128)S(1)}, f32[256,128]{1,0:T(8,128)S(1)}) custom-call(s32[7]{0:T(128)S(1)} %copy-done.8, bf16[2,256,256]{2,1,0:T(8,128)(2,1)S(1)} %pad_maximum_fusion.2.refs_0_, bf16[2,256,256]{2,1,0:T(8,128)(2,1)S(1)} %collective-permute-done.25.refs_1_, ...), custom_call_target="tpu_custom_call" | custom-call | tf_op jit(solution)/shard_map/mix_channels/pallas_call | solution.py:556
  220.7 5.0 %mix_channels.4 = (bf16[2,4,16,1024]{3,2,1,0:T(8,128)(2,1)S(1)}, bf16[2,4,16,1024]{3,2,1,0:T(8,128)(2,1)S(1)}, bf16[2,4,16,1024]{3,2,1,0:T(8,128)(2,1)S(1)}, bf16[2,4,16,1024]{3,2,1,0:T(8,128)(2,1)S(1)}) custom-call(s32[7]{0:T(128)S(1)} %copy-done.8, bf16[2,256,256]{2,1,0:T(8,128)(2,1)S(1)} %collective-permute-done.26.refs_0_, ...), custom_call_target="tpu_custom_call" | custom-call | tf_op jit(solution)/shard_map/mix_channels/pallas_call | solution.py:556
  227.8 4.9 %mix_channels.5 = (bf16[2,4,16,1024]{3,2,1,0:T(8,128)(2,1)S(1)}, bf16[2,4,16,1024]{3,2,1,0:T(8,128)(2,1)S(1)}, bf16[2,4,16,1024]{3,2,1,0:T(8,128)(2,1)S(1)}, bf16[2,4,16,1024]{3,2,1,0:T(8,128)(2,1)S(1)}) custom-call(s32[7]{0:T(128)S(1)} %copy-done.8, bf16[2,256,256]{2,1,0:T(8,128)(2,1)S(1)} %collective-permute-done.35.refs_0_, ...), custom_call_target="tpu_custom_call" | custom-call | tf_op jit(solution)/shard_map/mix_channels/pallas_call | solution.py:556
  237.1 4.5 %collective-permute-done.37 = bf16[2,4,16,1024]{3,2,1,0:T(8,128)(2,1)S(1)} collective-permute-done((bf16[2,4,16,1024]{3,2,1,0:T(8,128)(2,1)S(1)}, bf16[2,4,16,1024]{3,2,1,0:T(8,128)(2,1)S(1)}, u32[]{:S(2)}, u32[]{:S(2)}) %collective-permute-start.37) | collective-permute-done | bytes 262176 | tf_op jit(solution)/shard_map/ppermute | solution.py:173
  247.1 4.1 %collective-permute-start.42 = (bf16[4,16,1024]{2,1,0:T(8,128)(2,1)S(1)}, bf16[4,16,1024]{2,1,0:T(8,128)(2,1)S(1)}, u32[]{:S(2)}, u32[]{:S(2)}) collective-permute-start(bf16[4,16,1024]{2,1,0:T(8,128)(2,1)S(1)} %pad_maximum_fusion.5), channel_id=1, source_target_pairs={{0,16},{4,20},{8,24},{12,28},{16,0},{20,4},{24,8},{28,12},{1,17},{... | collective-permute-start | bytes 393224 | tf_op jit(solution)/shard_map/ppermute | solution.py:168
  253.9 2.8 %collective-permute-done.42 = bf16[4,16,1024]{2,1,0:T(8,128)(2,1)S(1)} collective-permute-done((bf16[4,16,1024]{2,1,0:T(8,128)(2,1)S(1)}, bf16[4,16,1024]{2,1,0:T(8,128)(2,1)S(1)}, u32[]{:S(2)}, u32[]{:S(2)}) %collective-permute-start.42) | collective-permute-done | bytes 131104 | tf_op jit(solution)/shard_map/ppermute | solution.py:168
  (195 shorter events, 53.2 us)
Async XLA Ops:
  0.0 13.3 %all-to-all-start = ((bf16[4,32,2048]{2,1,0:T(8,128)(2,1)}), bf16[4,32,2048]{2,1,0:T(8,128)(2,1)S(1)}, u32[]{:S(2)}, u32[]{:S(2)}) async-start(bf16[4,32,2048]{2,1,0:T(8,128)(2,1)} %bitcast.151), calls=%async_computation | async-start | bytes 1048576 | tf_op jit(solution)/shard_map/all_to_all | solution.py:659
  14.7 20.2 %all-to-all-start.1 = ((bf16[8,32,1024]{2,1,0:T(8,128)(2,1)}), bf16[8,32,1024]{2,1,0:T(8,128)(2,1)S(1)}, u32[]{:S(2)}, u32[]{:S(2)}) async-start(bf16[8,32,1024]{2,1,0:T(8,128)(2,1)} %bitcast.1), calls=%async_computation.1 | async-start | bytes 1048576 | tf_op jit(solution)/shard_map/all_to_all | solution.py:674
  44.3 27.7 %collective-permute-start = (bf16[4,560,256]{2,1,0:T(8,128)(2,1)}, bf16[4,560,256]{2,1,0:T(8,128)(2,1)S(1)}, u32[]{:S(2)}, u32[]{:S(2)}) collective-permute-start(bf16[4,560,256]{2,1,0:T(8,128)(2,1)} %get-tuple-element.44), channel_id=1, source_target_pairs={{0,4},{4,0},{8,12},{12,8},{16,20},{20,16},{24,28},{28,24},{1,5},{5... | collective-permute-start | bytes 3440648 | tf_op jit(solution)/shard_map/ppermute | solution.py:162
  44.4 14.5 %collective-permute-start.5 = (bf16[256,1024]{1,0:T(8,128)(2,1)}, bf16[256,1024]{1,0:T(8,128)(2,1)S(1)}, u32[]{:S(2)}, u32[]{:S(2)}) collective-permute-start(bf16[256,1024]{1,0:T(8,128)(2,1)} %bitcast.154), channel_id=1, source_target_pairs={{0,2},{1,3},{2,0},{3,1},{4,6},{5,7},{6,4},{7,5},{8,10},{9,11},{10,... | collective-permute-start | bytes 1572872 | tf_op jit(solution)/shard_map/ppermute | solution.py:173
  45.9 14.5 %collective-permute-start.4 = (bf16[256,1024]{1,0:T(8,128)(2,1)}, bf16[256,1024]{1,0:T(8,128)(2,1)S(1)}, u32[]{:S(2)}, u32[]{:S(2)}) collective-permute-start(bf16[256,1024]{1,0:T(8,128)(2,1)} %bitcast.155), channel_id=1, source_target_pairs={{0,1},{1,0},{2,3},{3,2},{4,5},{5,4},{6,7},{7,6},{8,9},{9,8},{10,11... | collective-permute-start | bytes 1572872 | tf_op jit(solution)/shard_map/ppermute | solution.py:173
  71.9 11.5 %collective-permute-start.12 = (bf16[4,400,256]{2,1,0:T(8,128)(2,1)S(1)}, bf16[4,400,256]{2,1,0:T(8,128)(2,1)S(1)}, u32[]{:S(2)}, u32[]{:S(2)}) collective-permute-start(bf16[4,400,256]{2,1,0:T(8,128)(2,1)S(1)} %get-tuple-element.49), channel_id=1, source_target_pairs={{0,4},{4,0},{8,12},{12,8},{16,20},{20,16},{24,28},{28,24},{1,5},{5... | collective-permute-start | bytes 2457608 | tf_op jit(solution)/shard_map/ppermute | solution.py:162
  72.1 11.1 %collective-permute-start.1 = (bf16[560,256]{1,0:T(8,128)(2,1)S(1)}, bf16[560,256]{1,0:T(8,128)(2,1)S(1)}, u32[]{:S(2)}, u32[]{:S(2)}) collective-permute-start(bf16[560,256]{1,0:T(8,128)(2,1)S(1)} %fusion.12), channel_id=1, source_target_pairs={{0,8},{4,12},{8,16},{12,20},{16,24},{20,28},{24,0},{28,4},{1,9},{5... | collective-permute-start | bytes 860168 | tf_op jit(solution)/shard_map/ppermute | solution.py:168
  77.1 31.7 %collective-permute-start.8 = (bf16[4,768,256]{2,1,0:T(8,128)(2,1)S(1)}, bf16[4,768,256]{2,1,0:T(8,128)(2,1)S(1)}, u32[]{:S(2)}, u32[]{:S(2)}) collective-permute-start(bf16[4,768,256]{2,1,0:T(8,128)(2,1)S(1)} %get-tuple-element.46), channel_id=1, source_target_pairs={{0,4},{4,0},{8,12},{12,8},{16,20},{20,16},{24,28},{28,24},{1,5},{5... | collective-permute-start | bytes 4718600 | tf_op jit(solution)/shard_map/ppermute | solution.py:162
  83.2 11.6 %collective-permute-start.2 = (bf16[560,256]{1,0:T(8,128)(2,1)S(1)}, bf16[560,256]{1,0:T(8,128)(2,1)S(1)}, u32[]{:S(2)}, u32[]{:S(2)}) collective-permute-start(bf16[560,256]{1,0:T(8,128)(2,1)S(1)} %fusion.5), channel_id=1, source_target_pairs={{0,8},{4,12},{8,16},{12,20},{16,24},{20,28},{24,0},{28,4},{1,9},{5... | collective-permute-start | bytes 860168 | tf_op jit(solution)/shard_map/ppermute | solution.py:168
  83.3 131.6 %collective-permute-start.28 = (bf16[2048,1024]{1,0:T(8,128)(2,1)}, bf16[2048,1024]{1,0:T(8,128)(2,1)}, u32[]{:S(2)}, u32[]{:S(2)}) collective-permute-start(bf16[2048,1024]{1,0:T(8,128)(2,1)} %refs_3_.7), channel_id=1, source_target_pairs={{0,4},{4,0},{8,12},{12,8},{16,20},{20,16},{24,28},{28,24},{1,5},{5... | collective-permute-start | bytes 12582920 | tf_op jit(solution)/shard_map/ppermute | solution.py:162
  83.5 15.5 %collective-permute-start.13 = (bf16[400,256]{1,0:T(8,128)(2,1)S(1)}, bf16[400,256]{1,0:T(8,128)(2,1)S(1)}, u32[]{:S(2)}, u32[]{:S(2)}) collective-permute-start(bf16[400,256]{1,0:T(8,128)(2,1)S(1)} %fusion.14), channel_id=1, source_target_pairs={{0,8},{4,12},{8,16},{12,20},{16,24},{20,28},{24,0},{28,4},{1,9},{5... | collective-permute-start | bytes 614408 | tf_op jit(solution)/shard_map/ppermute | solution.py:168
  98.9 19.8 %collective-permute-start.16 = (bf16[4,512,256]{2,1,0:T(8,128)(2,1)S(1)}, bf16[4,512,256]{2,1,0:T(8,128)(2,1)S(1)}, u32[]{:S(2)}, u32[]{:S(2)}) collective-permute-start(bf16[4,512,256]{2,1,0:T(8,128)(2,1)S(1)} %get-tuple-element.51), channel_id=1, source_target_pairs={{0,4},{4,0},{8,12},{12,8},{16,20},{20,16},{24,28},{28,24},{1,5},{5... | collective-permute-start | bytes 3145736 | tf_op jit(solution)/shard_map/ppermute | solution.py:162
  99.0 9.6 %collective-permute-start.14 = (bf16[400,256]{1,0:T(8,128)(2,1)S(1)}, bf16[400,256]{1,0:T(8,128)(2,1)S(1)}, u32[]{:S(2)}, u32[]{:S(2)}) collective-permute-start(bf16[400,256]{1,0:T(8,128)(2,1)S(1)} %fusion.9), channel_id=1, source_target_pairs={{0,8},{4,12},{8,16},{12,20},{16,24},{20,28},{24,0},{28,4},{1,9},{5... | collective-permute-start | bytes 614408 | tf_op jit(solution)/shard_map/ppermute | solution.py:168
  108.7 9.8 %collective-permute-start.15 = (bf16[400,256]{1,0:T(8,128)(2,1)S(1)}, bf16[400,256]{1,0:T(8,128)(2,1)S(1)}, u32[]{:S(2)}, u32[]{:S(2)}) collective-permute-start(bf16[400,256]{1,0:T(8,128)(2,1)S(1)} %fusion.10), channel_id=1, source_target_pairs={{0,8},{4,12},{8,16},{12,20},{16,24},{20,28},{24,0},{28,4},{1,9},{5... | collective-permute-start | bytes 614408 | tf_op jit(solution)/shard_map/ppermute | solution.py:168
  108.9 20.1 %collective-permute-start.9 = (bf16[768,256]{1,0:T(8,128)(2,1)S(1)}, bf16[768,256]{1,0:T(8,128)(2,1)S(1)}, u32[]{:S(2)}, u32[]{:S(2)}) collective-permute-start(bf16[768,256]{1,0:T(8,128)(2,1)S(1)} %fusion.11), channel_id=1, source_target_pairs={{0,8},{4,12},{8,16},{12,20},{16,24},{20,28},{24,0},{28,4},{1,9},{5... | collective-permute-start | bytes 1179656 | tf_op jit(solution)/shard_map/ppermute | solution.py:168
  118.6 10.5 %collective-permute-start.20 = (bf16[192,256]{1,0:T(8,128)(2,1)S(1)}, bf16[192,256]{1,0:T(8,128)(2,1)S(1)}, u32[]{:S(2)}, u32[]{:S(2)}) collective-permute-start(bf16[192,256]{1,0:T(8,128)(2,1)S(1)} %get-tuple-element.96), channel_id=1, source_target_pairs={{0,8},{4,12},{8,16},{12,20},{16,24},{20,28},{24,0},{28,4},{1,9},{5... | collective-permute-start | bytes 294920 | tf_op jit(solution)/shard_map/ppermute | solution.py:168
  118.8 18.0 %collective-permute-start.17 = (bf16[512,256]{1,0:T(8,128)(2,1)S(1)}, bf16[512,256]{1,0:T(8,128)(2,1)S(1)}, u32[]{:S(2)}, u32[]{:S(2)}) collective-permute-start(bf16[512,256]{1,0:T(8,128)(2,1)S(1)} %fusion.13), channel_id=1, source_target_pairs={{0,8},{4,12},{8,16},{12,20},{16,24},{20,28},{24,0},{28,4},{1,9},{5... | collective-permute-start | bytes 786440 | tf_op jit(solution)/shard_map/ppermute | solution.py:168
  129.2 18.3 %collective-permute-start.10 = (bf16[768,256]{1,0:T(8,128)(2,1)S(1)}, bf16[768,256]{1,0:T(8,128)(2,1)S(1)}, u32[]{:S(2)}, u32[]{:S(2)}) collective-permute-start(bf16[768,256]{1,0:T(8,128)(2,1)S(1)} %fusion.3), channel_id=1, source_target_pairs={{0,8},{4,12},{8,16},{12,20},{16,24},{20,28},{24,0},{28,4},{1,9},{5... | collective-permute-start | bytes 1179656 | tf_op jit(solution)/shard_map/ppermute | solution.py:168
  136.8 10.5 %collective-permute-start.22 = (bf16[192,256]{1,0:T(8,128)(2,1)S(1)}, bf16[192,256]{1,0:T(8,128)(2,1)S(1)}, u32[]{:S(2)}, u32[]{:S(2)}) collective-permute-start(bf16[192,256]{1,0:T(8,128)(2,1)S(1)} %collective-permute-done.21), channel_id=1, source_target_pairs={{0,8},{4,12},{8,16},{12,20},{16,24},{20,28},{24,0},{28,4},{1,9},{5... | collective-permute-start | bytes 294920 | tf_op jit(solution)/shard_map/ppermute | solution.py:168
  136.9 15.0 %collective-permute-start.18 = (bf16[512,256]{1,0:T(8,128)(2,1)S(1)}, bf16[512,256]{1,0:T(8,128)(2,1)S(1)}, u32[]{:S(2)}, u32[]{:S(2)}) collective-permute-start(bf16[512,256]{1,0:T(8,128)(2,1)S(1)} %fusion.7), channel_id=1, source_target_pairs={{0,8},{4,12},{8,16},{12,20},{16,24},{20,28},{24,0},{28,4},{1,9},{5... | collective-permute-start | bytes 786440 | tf_op jit(solution)/shard_map/ppermute | solution.py:168
  147.4 19.2 %collective-permute-start.23 = (bf16[4,192,256]{2,1,0:T(8,128)(2,1)S(1)}, bf16[4,192,256]{2,1,0:T(8,128)(2,1)S(1)}, u32[]{:S(2)}, u32[]{:S(2)}) collective-permute-start(bf16[4,192,256]{2,1,0:T(8,128)(2,1)S(1)} %pad_maximum_fusion.1.refs_9_), channel_id=1, source_target_pairs={{0,4},{4,0},{8,12},{12,8},{16,20},{20,16},{24,28},{28,24},{1,5},{5... | collective-permute-start | bytes 1179656 | tf_op jit(solution)/shard_map/ppermute | solution.py:162
  147.6 32.3 %collective-permute-start.11 = (bf16[768,256]{1,0:T(8,128)(2,1)S(1)}, bf16[768,256]{1,0:T(8,128)(2,1)S(1)}, u32[]{:S(2)}, u32[]{:S(2)}) collective-permute-start(bf16[768,256]{1,0:T(8,128)(2,1)S(1)} %fusion.4), channel_id=1, source_target_pairs={{0,8},{4,12},{8,16},{12,20},{16,24},{20,28},{24,0},{28,4},{1,9},{5... | collective-permute-start | bytes 1179656 | tf_op jit(solution)/shard_map/ppermute | solution.py:168
  152.0 14.6 %collective-permute-start.19 = (bf16[512,256]{1,0:T(8,128)(2,1)S(1)}, bf16[512,256]{1,0:T(8,128)(2,1)S(1)}, u32[]{:S(2)}, u32[]{:S(2)}) collective-permute-start(bf16[512,256]{1,0:T(8,128)(2,1)S(1)} %fusion.8), channel_id=1, source_target_pairs={{0,8},{4,12},{8,16},{12,20},{16,24},{20,28},{24,0},{28,4},{1,9},{5... | collective-permute-start | bytes 786440 | tf_op jit(solution)/shard_map/ppermute | solution.py:168
  187.0 11.0 %collective-permute-start.25 = (bf16[2,256,256]{2,1,0:T(8,128)(2,1)S(1)}, bf16[2,256,256]{2,1,0:T(8,128)(2,1)S(1)}, u32[]{:S(2)}, u32[]{:S(2)}) collective-permute-start(bf16[2,256,256]{2,1,0:T(8,128)(2,1)S(1)} %pad_maximum_fusion.2.refs_0_), channel_id=1, source_target_pairs={{0,8},{4,12},{8,16},{12,20},{16,24},{20,28},{24,0},{28,4},{1,9},{5... | collective-permute-start | bytes 786440 | tf_op jit(solution)/shard_map/ppermute | solution.py:168
  189.6 14.1 %collective-permute-start.30 = (bf16[2,256,256]{2,1,0:T(8,128)(2,1)S(1)}, bf16[2,256,256]{2,1,0:T(8,128)(2,1)}, u32[]{:S(2)}, u32[]{:S(2)}) collective-permute-start(bf16[2,256,256]{2,1,0:T(8,128)(2,1)S(1)} %pad_maximum_fusion.3.refs_2_), channel_id=1, source_target_pairs={{0,8},{4,12},{8,16},{12,20},{16,24},{20,28},{24,0},{28,4},{1,9},{5... | collective-permute-start | bytes 786440 | tf_op jit(solution)/shard_map/ppermute | solution.py:168
  198.0 11.2 %collective-permute-start.26 = (bf16[2,256,256]{2,1,0:T(8,128)(2,1)S(1)}, bf16[2,256,256]{2,1,0:T(8,128)(2,1)S(1)}, u32[]{:S(2)}, u32[]{:S(2)}) collective-permute-start(bf16[2,256,256]{2,1,0:T(8,128)(2,1)S(1)} %collective-permute-done.25.refs_1_), channel_id=1, source_target_pairs={{0,8},{4,12},{8,16},{12,20},{16,24},{20,28},{24,0},{28,4},{1,9},{5... | collective-permute-start | bytes 786440 | tf_op jit(solution)/shard_map/ppermute | solution.py:168
  203.7 11.2 %collective-permute-start.35 = (bf16[2,256,256]{2,1,0:T(8,128)(2,1)}, bf16[2,256,256]{2,1,0:T(8,128)(2,1)S(1)}, u32[]{:S(2)}, u32[]{:S(2)}) collective-permute-start(bf16[2,256,256]{2,1,0:T(8,128)(2,1)} %collective-permute-done.30.refs_3_), channel_id=1, source_target_pairs={{0,8},{4,12},{8,16},{12,20},{16,24},{20,28},{24,0},{28,4},{1,9},{5... | collective-permute-start | bytes 786440 | tf_op jit(solution)/shard_map/ppermute | solution.py:168
  209.3 11.4 %collective-permute-start.27 = (bf16[2,256,256]{2,1,0:T(8,128)(2,1)S(1)}, bf16[2,256,256]{2,1,0:T(8,128)(2,1)}, u32[]{:S(2)}, u32[]{:S(2)}) collective-permute-start(bf16[2,256,256]{2,1,0:T(8,128)(2,1)S(1)} %collective-permute-done.26.refs_0_), channel_id=1, source_target_pairs={{0,8},{4,12},{8,16},{12,20},{16,24},{20,28},{24,0},{28,4},{1,9},{5... | collective-permute-start | bytes 786440 | tf_op jit(solution)/shard_map/ppermute | solution.py:168
  214.9 12.9 %collective-permute-start.36 = (bf16[2,256,256]{2,1,0:T(8,128)(2,1)S(1)}, bf16[2,256,256]{2,1,0:T(8,128)(2,1)S(1)}, u32[]{:S(2)}, u32[]{:S(2)}) collective-permute-start(bf16[2,256,256]{2,1,0:T(8,128)(2,1)S(1)} %collective-permute-done.35.refs_0_), channel_id=1, source_target_pairs={{0,8},{4,12},{8,16},{12,20},{16,24},{20,28},{24,0},{28,4},{1,9},{5... | collective-permute-start | bytes 786440 | tf_op jit(solution)/shard_map/ppermute | solution.py:168
  225.7 9.1 %collective-permute-start.31 = (bf16[2,4,16,1024]{3,2,1,0:T(8,128)(2,1)S(1)}, bf16[2,4,16,1024]{3,2,1,0:T(8,128)(2,1)S(1)}, u32[]{:S(2)}, u32[]{:S(2)}) collective-permute-start(bf16[2,4,16,1024]{3,2,1,0:T(8,128)(2,1)S(1)} %get-tuple-element.64), channel_id=1, source_target_pairs={{0,1},{1,0},{2,3},{3,2},{4,5},{5,4},{6,7},{7,6},{8,9},{9,8},{10,11... | collective-permute-start | bytes 786440 | tf_op jit(solution)/shard_map/ppermute | solution.py:173
  226.3 9.1 %collective-permute-start.33 = (bf16[2,4,16,1024]{3,2,1,0:T(8,128)(2,1)S(1)}, bf16[2,4,16,1024]{3,2,1,0:T(8,128)(2,1)S(1)}, u32[]{:S(2)}, u32[]{:S(2)}) collective-permute-start(bf16[2,4,16,1024]{3,2,1,0:T(8,128)(2,1)S(1)} %get-tuple-element.66), channel_id=1, source_target_pairs={{0,2},{1,3},{2,0},{3,1},{4,6},{5,7},{6,4},{7,5},{8,10},{9,11},{10,... | collective-permute-start | bytes 786440 | tf_op jit(solution)/shard_map/ppermute | solution.py:173
  247.1 9.6 %collective-permute-start.42 = (bf16[4,16,1024]{2,1,0:T(8,128)(2,1)S(1)}, bf16[4,16,1024]{2,1,0:T(8,128)(2,1)S(1)}, u32[]{:S(2)}, u32[]{:S(2)}) collective-permute-start(bf16[4,16,1024]{2,1,0:T(8,128)(2,1)S(1)} %pad_maximum_fusion.5), channel_id=1, source_target_pairs={{0,16},{4,20},{8,24},{12,28},{16,0},{20,4},{24,8},{28,12},{1,17},{... | collective-permute-start | bytes 393224 | tf_op jit(solution)/shard_map/ppermute | solution.py:168
  (45 other events, 686.4 us)
